TPU v7x, 512 devices: a whole 4x8x8 slice. The times are simulated.
512 devices in a mesh: ab: 32 (over z, x), cd: 16 (over y, core).
Axes of the slice: x: 4, y: 8, z: 8, core: 2. Of those that a mesh axis runs over, the one named last changes fastest.
Arguments:
- amplitudes: float32 [512, 8192], P('ab', 'cd'), may hold values from -6 to 6
- integrals: float32 [65536, 8192], P('ab', 'cd'), may hold values from -0.125 to 0.125
- ij_pairs: int32 [512, 2], P('cd'), may hold values from 0 to 127
- ab_pairs: int32 [65536, 2], P('ab'), may hold values from 0 to 1535
- eps_occ: float32 [128], replicated, may hold values from -1.5 to -0.3
- eps_vir: float32 [1536], replicated, may hold values from 0.1 to 2.5
Outputs:
- ladder: float32 [512, 65536], P('cd', 'ab')
- update: float32 [512, 65536], P('cd', 'ab')
All inputs are finite; a program needn't handle non-finite values.
Results may differ from a plain program's by a relative error of at most 0.00015.
Values sent between devices are 32-bit elements; how exact they have to be, the bound alone decides.
A program may use at most 64 MiB of HBM per device.

v0:
```python
import jax
import jax.numpy as jnp
from jax import lax
from jax.sharding import PartitionSpec as P


def lookup_energy(indices, energies):
    positions = lax.broadcasted_iota(jnp.int32, (indices.shape[0], energies.shape[0]), 1)
    picked = jnp.where(indices[:, None] == positions, energies[None, :], jnp.float32(0.0))
    return jnp.sum(picked, axis=1)


def contract_rows(row_block, col_block):
    return lax.dot_general(
        row_block,
        col_block,
        (((1,), (1,)), ((), ())),
        precision=lax.Precision.HIGHEST,
        preferred_element_type=jnp.float32,
    )


def on_device(amplitudes, integrals, ij_pairs, ab_pairs, eps_occ, eps_vir):
    partial_value = contract_rows(lax.all_gather(amplitudes, "ab", axis=0, tiled=True), integrals)
    ladder = lax.psum_scatter(partial_value, "cd", scatter_dimension=0, tiled=True)
    first_occ = lookup_energy(ij_pairs[:, 0], eps_occ)[:, None]
    second_occ = lookup_energy(ij_pairs[:, 1], eps_occ)[:, None]
    first_vir = lookup_energy(ab_pairs[:, 0], eps_vir)[None, :]
    second_vir = lookup_energy(ab_pairs[:, 1], eps_vir)[None, :]
    denominator = first_occ + second_occ - first_vir - second_vir
    update = ladder / denominator
    return (ladder, update)


def solution(mesh):
    in_specs = (P("ab", "cd"), P("ab", "cd"), P("cd", None), P("ab", None), P(), P())
    out_specs = (P("cd", "ab"), P("cd", "ab"))
    return jax.shard_map(
        on_device, mesh=mesh, in_specs=in_specs, out_specs=out_specs, check_vma=False
    )
```

profile of v0, /device:TPU:1, one launch (start us, length us, event | category | flops | bytes accessed | tf_op | source)
XLA Modules:
  0.0 178.5 jit_solution(8097404686899207612)
XLA Ops:
  7.2 0.0 all-gather.2.cloned.1.call-start
  7.2 0.7 all-gather.2.cloned.1.call-update
  7.9 0.0 reduce-scatter.2.cloned.1.call-start
  7.9 86.6 %all-gather.2.cloned.1.call-done = f32[512,512]{1,0:T(8,128)} async-done(((f32[16,512]{1,0:T(8,128)}), f32[512,512]{1,0:T(8,128)}) %all-gather.2.cloned.1.call-update) | async-done | bytes 1048592 | tf_op jit(solution)/shard_map/all_gather | solution.py:24
  94.5 10.4 %fusion.1 = f32[512,2048]{1,0:T(8,128)} fusion(f32[512,512]{1,0:T(8,128)} %all-gather.2.cloned.1.call-done, f32[2048,512]{1,0:T(8,128)} %param.7), kind=kOutput, calls=%fused_computation.12 | convolution fusion | flops 6442450944 | bytes 9437184 | tf_op jit(solution)/shard_map/dot_general | solution.py:14
  104.9 0.0 copy-start.1
  104.9 0.0 copy-start.2
  104.9 0.0 copy-start
  104.9 0.0 copy-start.3
  104.9 0.0 reduce-scatter.2.cloned.1.call-update
  104.9 0.6 copy-done.1
  105.5 0.0 copy-done.2
  105.5 0.2 select_reduce_fusion.2
  105.7 0.0 copy-done
  105.8 0.0 copy-done.3
  105.8 3.9 %select_reduce_fusion.1 = (f32[2048]{0:T(1024)S(1)}, f32[2048]{0:T(1024)S(1)}) fusion(f32[1536]{0:T(1024)S(1)} %copy-done.3, s32[2048]{0:T(1024)S(1)} %bitcast.9, s32[2048]{0:T(1024)S(1)} %bitcast.8), kind=kLoop, calls=%fused_computation.2 | loop fusion | flops 18870272 | bytes 38912 | tf_op jit(solution)/shard_map/reduce_sum | solution.py:10
  109.7 60.2 %reduce-scatter.2.cloned.1.call-done = f32[32,2048]{1,0:T(8,128)} async-done(((f32[512,2048]{1,0:T(8,128)}), f32[32,2048]{1,0:T(8,128)}) %reduce-scatter.2.cloned.1.call-update) | async-done | bytes 262160 | tf_op jit(solution)/shard_map/reduce_scatter | solution.py:25
  169.9 1.8 subtract_divide_fusion
  (3 shorter events, 0.0 us)
Async XLA Ops:
  7.2 87.3 %all-gather.2.cloned.1.call-start = ((), (), s32[]{:S(2)}) async-start(), calls=%async_computation.1 | async-start | bytes 1081344 | tf_op jit(solution)/shard_map/all_gather | solution.py:24
  7.9 162.0 %reduce-scatter.2.cloned.1.call-start = ((), (), s32[]{:S(2)}) async-start(), calls=%async_computation.2 | async-start | bytes 4456448 | tf_op jit(solution)/shard_map/reduce_scatter | solution.py:25
  104.9 0.7 copy-start.1
  104.9 0.7 copy-start.2
  104.9 0.9 copy-start
  104.9 0.9 copy-start.3
Sparse Core Ops, SparseCore 0:
  11.2 83.2 all-gather.1
  105.0 64.8 reduce-scatter.1
where the time goes:
time: 180 us; the launch traced here: 179 us
  waiting for transfers between devices  147 us (82%)
  between operations  14.1 us (8%)
  matrix products  10.4 us (6%)
  other arithmetic  5.86 us (3%)
    all_gather x1, waiting for transfers between devices, on_device(): lax.all_gather(amplitudes, 'ab', axis=0, tiled=True)  86.6 us
    reduce_scatter x1, waiting for transfers between devices, on_device(): lax.psum_scatter(partial_value, 'cd', scatter_dimension=0, tiled=True)  60.2 us
    dot_general x1, matrix products, contract_rows(): lax.dot_general(row_block, col_block, (((1,), (1,)), ((), ())), precision...  10.4 us
    reduce_sum x2, other arithmetic, lookup_energy(): return jnp.sum(picked, axis=1)  4.09 us
  transfers between devices with their start and end apart: 2, of which 2 were waited for; matrix products, arithmetic and copies ran while one was open for 2% of the time, Pallas kernels for 0%

commit v1 on v0

--- a/solution.py
+++ b/solution.py
@@ -1,7 +1,13 @@
+import functools
+
 import jax
 import jax.numpy as jnp
 from jax import lax
+from jax.experimental import pallas as pl
+from jax.experimental.pallas import tpu as pltpu
 from jax.sharding import PartitionSpec as P
+
+MESH = pl.DeviceIdType.MESH
 
 
 def lookup_energy(indices, energies):
@@ -20,8 +26,78 @@
     )
 
 
-def on_device(amplitudes, integrals, ij_pairs, ab_pairs, eps_occ, eps_vir):
-    partial_value = contract_rows(lax.all_gather(amplitudes, "ab", axis=0, tiled=True), integrals)
+def gather_kernel(n, amp_ref, out_ref, held, send_sems, recv_sems):
+    me = lax.axis_index("ab")
+    cd = lax.axis_index("cd")
+    rows = amp_ref.shape[0]
+
+    barrier = pltpu.get_barrier_semaphore()
+
+    def greet(i, carry):
+        peer = lax.rem(me + i, n)
+        pl.semaphore_signal(barrier, inc=1, device_id=(peer, cd), device_id_type=MESH)
+        return carry
+
+    lax.fori_loop(1, n, greet, 0)
+    pl.semaphore_wait(barrier, n - 1)
+
+    mine = pl.ds(pl.multiple_of(me * rows, rows), rows)
+
+    def copy_to(peer):
+        return pltpu.make_async_remote_copy(
+            src_ref=amp_ref,
+            dst_ref=held.at[mine],
+            send_sem=send_sems.at[peer],
+            recv_sem=recv_sems.at[me],
+            device_id=(peer, cd),
+            device_id_type=MESH,
+        )
+
+    def copy_from(peer):
+        theirs = pl.ds(pl.multiple_of(peer * rows, rows), rows)
+        return pltpu.make_async_remote_copy(
+            src_ref=amp_ref,
+            dst_ref=held.at[theirs],
+            send_sem=send_sems.at[peer],
+            recv_sem=recv_sems.at[peer],
+            device_id=(peer, cd),
+            device_id_type=MESH,
+        )
+
+    def send(i, carry):
+        copy_to(lax.rem(me + i, n)).start()
+        return carry
+
+    lax.fori_loop(1, n, send, 0)
+    held[mine, :] = amp_ref[...]
+
+    def finish(i, carry):
+        copy_to(lax.rem(me + i, n)).wait_send()
+        copy_from(lax.rem(me + n - i, n)).wait_recv()
+        return carry
+
+    lax.fori_loop(1, n, finish, 0)
+    out_ref[...] = held[...]
+
+
+def gather_rows(amplitudes, n):
+    rows, cols = amplitudes.shape
+    return pl.pallas_call(
+        functools.partial(gather_kernel, n),
+        out_shape=jax.ShapeDtypeStruct((rows * n, cols), amplitudes.dtype),
+        in_specs=[pl.BlockSpec(memory_space=pltpu.VMEM)],
+        out_specs=pl.BlockSpec(memory_space=pltpu.VMEM),
+        scratch_shapes=[
+            pltpu.VMEM((rows * n, cols), amplitudes.dtype),
+            pltpu.SemaphoreType.DMA((n,)),
+            pltpu.SemaphoreType.DMA((n,)),
+        ],
+        compiler_params=pltpu.CompilerParams(collective_id=0, has_side_effects=True),
+    )(amplitudes)
+
+
+def on_device(n_ab, amplitudes, integrals, ij_pairs, ab_pairs, eps_occ, eps_vir):
+    partial_value = contract_rows(gather_rows(amplitudes, n_ab), integrals)
     ladder = lax.psum_scatter(partial_value, "cd", scatter_dimension=0, tiled=True)
     first_occ = lookup_energy(ij_pairs[:, 0], eps_occ)[:, None]
     second_occ = lookup_energy(ij_pairs[:, 1], eps_occ)[:, None]
@@ -36,5 +112,9 @@
     in_specs = (P("ab", "cd"), P("ab", "cd"), P("cd", None), P("ab", None), P(), P())
     out_specs = (P("cd", "ab"), P("cd", "ab"))
     return jax.shard_map(
-        on_device, mesh=mesh, in_specs=in_specs, out_specs=out_specs, check_vma=False
+        functools.partial(on_device, mesh.shape["ab"]),
+        mesh=mesh,
+        in_specs=in_specs,
+        out_specs=out_specs,
+        check_vma=False,
     )

time: 180 us -> 131 us (0.73)
  waiting for transfers between devices: 147 us -> 61.6 us
  Pallas kernels: 0 us -> 36.9 us
    all_gather x1 -> x0, waiting for transfers between devices: 86.6 us -> none  [on_device(): lax.all_gather(amplitudes, 'ab', axis=0, tiled=True)]
    pallas_call x0 -> x1, Pallas kernels: none -> 36.9 us  [gather_rows(): pl.pallas_call(functools.partial(gather_kernel, n), out_shape=jax.ShapeDt...]
  transfers between devices with their start and end apart: 2 -> 1, of which waited for: 2 -> 1; matrix products, arithmetic and copies ran while one was open for 2% -> 3% of each run, Pallas kernels for 0% -> 0%
where the time goes in v1:
time: 131 us; the launch traced here: 130 us
  waiting for transfers between devices  61.6 us (47%)
  Pallas kernels  36.9 us (28%)
  between operations  14.1 us (11%)
  matrix products  10.4 us (8%)
  other arithmetic  5.86 us (4%)
    reduce_scatter x1, waiting for transfers between devices, on_device(): lax.psum_scatter(partial_value, 'cd', scatter_dimension=0, tiled=True)  61.6 us
    pallas_call x1, Pallas kernels, gather_rows(): pl.pallas_call(functools.partial(gather_kernel, n), out_shape=jax.ShapeDt...  36.9 us
    dot_general x1, matrix products, contract_rows(): lax.dot_general(row_block, col_block, (((1,), (1,)), ((), ())), precision...  10.4 us
    reduce_sum x2, other arithmetic, lookup_energy(): return jnp.sum(picked, axis=1)  4.09 us
  transfers between devices with their start and end apart: 1, of which 1 were waited for; matrix products, arithmetic and copies ran while one was open for 3% of the time, Pallas kernels for 0%

profile of v1, /device:TPU:1, one launch (start us, length us, event | category | flops | bytes accessed | tf_op | source)
XLA Modules:
  0.0 129.5 jit_solution(14216957137388286843)
XLA Ops:
  7.2 0.0 reduce-scatter.2.cloned.1.call-start
  7.2 36.9 %shard_map.77 = f32[512,512]{1,0:T(8,128)} custom-call(f32[16,512]{1,0:T(8,128)} %amp_ref.1), custom_call_target="tpu_custom_call" | custom-call | tf_op jit(solution)/shard_map/pallas_call | solution.py:85
  44.1 10.4 %fusion.1 = f32[512,2048]{1,0:T(8,128)} fusion(f32[512,512]{1,0:T(8,128)} %shard_map.77, f32[2048,512]{1,0:T(8,128)} %param.7), kind=kOutput, calls=%fused_computation.12 | convolution fusion | flops 6442450944 | bytes 9437184 | tf_op jit(solution)/shard_map/dot_general | solution.py:20
  54.5 0.0 copy-start.1
  54.5 0.0 copy-start.2
  54.5 0.0 copy-start
  54.5 0.0 copy-start.3
  54.5 0.0 reduce-scatter.2.cloned.1.call-update
  54.5 0.6 copy-done.1
  55.2 0.0 copy-done.2
  55.2 0.2 select_reduce_fusion.2
  55.4 0.0 copy-done
  55.4 0.0 copy-done.3
  55.4 3.9 %select_reduce_fusion.1 = (f32[2048]{0:T(1024)S(1)}, f32[2048]{0:T(1024)S(1)}) fusion(f32[1536]{0:T(1024)S(1)} %copy-done.3, s32[2048]{0:T(1024)S(1)} %bitcast.9, s32[2048]{0:T(1024)S(1)} %bitcast.8), kind=kLoop, calls=%fused_computation.2 | loop fusion | flops 18870272 | bytes 38912 | tf_op jit(solution)/shard_map/reduce_sum | solution.py:16
  59.3 61.6 %reduce-scatter.2.cloned.1.call-done = f32[32,2048]{1,0:T(8,128)} async-done(((f32[512,2048]{1,0:T(8,128)}), f32[32,2048]{1,0:T(8,128)}) %reduce-scatter.2.cloned.1.call-update) | async-done | bytes 262160 | tf_op jit(solution)/shard_map/reduce_scatter | solution.py:101
  120.9 1.8 %subtract_divide_fusion = f32[32,2048]{1,0:T(8,128)} fusion(f32[32,2048]{1,0:T(8,128)} %reduce-scatter.2.cloned.1.call-done, f32[2048]{0:T(1024)S(1)} %get-tuple-element.3, f32[2048]{0:T(1024)S(1)} %get-tuple-element.2, f32[32]{0:T(128)S(1)} %add.10), kind=kLoop, calls=%fused_computation.4 | loop fusion | flops 196608 | bytes 540800 | tf_op jit(solution)/shard_map/div | solution.py:107
  (3 shorter events, 0.0 us)
Async XLA Ops:
  7.2 113.8 %reduce-scatter.2.cloned.1.call-start = ((), (), s32[]{:S(2)}) async-start(), calls=%async_computation.1 | async-start | bytes 4456448 | tf_op jit(solution)/shard_map/reduce_scatter | solution.py:101
  54.5 0.7 copy-start.1
  54.5 0.7 copy-start.2
  54.5 0.9 copy-start
  54.5 0.9 copy-start.3
Sparse Core Ops, SparseCore 0:
  54.7 66.2 reduce-scatter.1

commit v2 on v1

--- a/solution.py
+++ b/solution.py
@@ -96,9 +96,121 @@
     )(amplitudes)
 
 
-def on_device(n_ab, amplitudes, integrals, ij_pairs, ab_pairs, eps_occ, eps_vir):
+def scatter_kernel(n_y, part_ref, out_ref, pair, send_r, recv_r, send_l, recv_l,
+                   pair_send, pair_recv, ring_send, ring_recv):
+    ab = lax.axis_index("ab")
+    cd = lax.axis_index("cd")
+    y, core = cd // 2, lax.rem(cd, 2)
+    other = 1 - core
+    right = lax.rem(y + 1, n_y) * 2 + core
+    left = lax.rem(y + n_y - 1, n_y) * 2 + core
+    partner = y * 2 + other
+    half = out_ref.shape[1] // 2
+
+    barrier = pltpu.get_barrier_semaphore()
+    for peer in (partner, right, left):
+        pl.semaphore_signal(barrier, inc=1, device_id=(ab, peer), device_id_type=MESH)
+    pl.semaphore_wait(barrier, 3)
+
+    order = []
+    for k in list(range(1, n_y // 2 + 1)) + [0]:
+        for sign in (1, -1):
+            if (sign * k) % n_y not in [j % n_y for j in order]:
+                order.append(sign * k)
+
+    def pair_copy(k):
+        b = lax.rem(y + k + n_y, n_y)
+        return pltpu.make_async_remote_copy(
+            src_ref=part_ref.at[b, other],
+            dst_ref=pair.at[b],
+            send_sem=pair_send.at[b],
+            recv_sem=pair_recv.at[b],
+            device_id=(ab, partner),
+            device_id_type=MESH,
+        )
+
+    for k in order:
+        pair_copy(k).start()
+
+    def own(k, cols):
+        b = lax.rem(y + k + n_y, n_y)
+        return part_ref[b, core, :, cols] + pair[b, :, cols]
+
+    lo, hi = slice(0, half), slice(half, 2 * half)
+
+    def ring_copy(d, s):
+        src, dst = (send_r, recv_r) if d == 0 else (send_l, recv_l)
+        return pltpu.make_async_remote_copy(
+            src_ref=src.at[s],
+            dst_ref=dst.at[s],
+            send_sem=ring_send.at[d, s],
+            recv_sem=ring_recv.at[d, s],
+            device_id=(ab, right if d == 0 else left),
+            device_id_type=MESH,
+        )
+
+    waited = set()
+
+    def need(k):
+        k = k % n_y
+        if k not in waited:
+            waited.add(k)
+            pair_copy(k if k <= n_y // 2 else k - n_y).wait_recv()
+
+    for s in range(n_y - 1):
+        need(-(s + 1))
+        need(s + 1)
+        if s == 0:
+            send_r[s] = own(-1, lo)
+            send_l[s] = own(1, hi)
+        else:
+            ring_copy(0, s - 1).wait_recv()
+            send_r[s] = recv_r[s - 1] + own(-(s + 1), lo)
+            ring_copy(1, s - 1).wait_recv()
+            send_l[s] = recv_l[s - 1] + own(s + 1, hi)
+        ring_copy(0, s).start()
+        ring_copy(1, s).start()
+    need(0)
+    ring_copy(0, n_y - 2).wait_recv()
+    out_ref[:, lo] = recv_r[n_y - 2] + own(0, lo)
+    ring_copy(1, n_y - 2).wait_recv()
+    out_ref[:, hi] = recv_l[n_y - 2] + own(0, hi)
+    for k in order:
+        pair_copy(k).wait_send()
+    for s in range(n_y - 1):
+        ring_copy(0, s).wait_send()
+        ring_copy(1, s).wait_send()
+
+
+def scatter_rows(partial_value, n_cd):
+    n_y = n_cd // 2
+    total_rows, cols = partial_value.shape
+    rows = total_rows // n_cd
+    blocks = partial_value.reshape(n_y, 2, rows, cols)
+    half = cols // 2
+    return pl.pallas_call(
+        functools.partial(scatter_kernel, n_y),
+        out_shape=jax.ShapeDtypeStruct((rows, cols), partial_value.dtype),
+        in_specs=[pl.BlockSpec(memory_space=pltpu.VMEM)],
+        out_specs=pl.BlockSpec(memory_space=pltpu.VMEM),
+        scratch_shapes=[
+            pltpu.VMEM((n_y, rows, cols), jnp.float32),
+            pltpu.VMEM((n_y - 1, rows, half), jnp.float32),
+            pltpu.VMEM((n_y - 1, rows, half), jnp.float32),
+            pltpu.VMEM((n_y - 1, rows, half), jnp.float32),
+            pltpu.VMEM((n_y - 1, rows, half), jnp.float32),
+            pltpu.SemaphoreType.DMA((n_y,)),
+            pltpu.SemaphoreType.DMA((n_y,)),
+            pltpu.SemaphoreType.DMA((2, n_y - 1)),
+            pltpu.SemaphoreType.DMA((2, n_y - 1)),
+        ],
+        compiler_params=pltpu.CompilerParams(collective_id=1, has_side_effects=True),
+    )(blocks)
+
+
+def on_device(n_ab, n_cd, amplitudes, integrals, ij_pairs, ab_pairs, eps_occ, eps_vir):
     partial_value = contract_rows(gather_rows(amplitudes, n_ab), integrals)
-    ladder = lax.psum_scatter(partial_value, "cd", scatter_dimension=0, tiled=True)
+    ladder = scatter_rows(partial_value, n_cd)
     first_occ = lookup_energy(ij_pairs[:, 0], eps_occ)[:, None]
     second_occ = lookup_energy(ij_pairs[:, 1], eps_occ)[:, None]
     first_vir = lookup_energy(ab_pairs[:, 0], eps_vir)[None, :]
@@ -112,7 +224,7 @@
     in_specs = (P("ab", "cd"), P("ab", "cd"), P("cd", None), P("ab", None), P(), P())
     out_specs = (P("cd", "ab"), P("cd", "ab"))
     return jax.shard_map(
-        functools.partial(on_device, mesh.shape["ab"]),
+        functools.partial(on_device, mesh.shape["ab"], mesh.shape["cd"]),
         mesh=mesh,
         in_specs=in_specs,
         out_specs=out_specs,

time: 131 us -> 102 us (0.78)
  the two profiles are of different devices: /device:TPU:1 before, /device:TPU:6 now
where the time goes in v2:
time: 102 us
  Pallas kernels  83.5 us (82%)
  matrix products  10.4 us (10%)
  other arithmetic  5.87 us (6%)
  local copies, waits for them, and re-layouts  1.71 us (2%)
    pallas_call x1, Pallas kernels, scatter_rows(): pl.pallas_call(functools.partial(scatter_kernel, n_y), out_shape=jax.Shap...  43.9 us
    pallas_call x1, Pallas kernels, gather_rows(): pl.pallas_call(functools.partial(gather_kernel, n), out_shape=jax.ShapeDt...  39.6 us
    dot_general x1, matrix products, contract_rows(): lax.dot_general(row_block, col_block, (((1,), (1,)), ((), ())), precision...  10.4 us
    reduce_sum x2, other arithmetic, lookup_energy(): return jnp.sum(picked, axis=1)  4.09 us

profile of v2, /device:TPU:6, one launch (start us, length us, event | category | flops | bytes accessed | tf_op | source)
XLA Modules:
  0.0 102.1 jit_solution(3161944635727051183)
XLA Ops:
  0.6 39.6 %shard_map.77 = f32[512,512]{1,0:T(8,128)} custom-call(f32[16,512]{1,0:T(8,128)} %amp_ref.1), custom_call_target="tpu_custom_call" | custom-call | tf_op jit(solution)/shard_map/pallas_call | solution.py:85
  40.2 10.4 %fusion.1 = f32[512,2048]{1,0:T(8,128)} fusion(f32[512,512]{1,0:T(8,128)} %shard_map.77, f32[2048,512]{1,0:T(8,128)} %param.7), kind=kOutput, calls=%fused_computation.12 | convolution fusion | flops 6442450944 | bytes 9437184 | tf_op jit(solution)/shard_map/dot_general | solution.py:20
  50.6 0.0 copy-start
  50.6 0.0 copy-start.3
  50.6 0.0 copy-start.1
  50.6 0.0 copy-start.2
  50.6 43.9 %shard_map.78 = f32[32,2048]{1,0:T(8,128)} custom-call(f32[8,2,32,2048]{3,2,1,0:T(8,128)} %bitcast.9), custom_call_target="tpu_custom_call" | custom-call | tf_op jit(solution)/shard_map/pallas_call | solution.py:191
  94.5 0.0 copy-done
  94.6 0.0 copy-done.3
  94.6 3.9 %select_reduce_fusion.1 = (f32[2048]{0:T(1024)S(1)}, f32[2048]{0:T(1024)S(1)}) fusion(f32[1536]{0:T(1024)S(1)} %copy-done.3, s32[2048]{0:T(1024)S(1)} %bitcast.11, s32[2048]{0:T(1024)S(1)} %bitcast.10), kind=kLoop, calls=%fused_computation.2 | loop fusion | flops 18870272 | bytes 38912 | tf_op jit(solution)/shard_map/reduce_sum | solution.py:16
  98.5 0.0 copy-done.1
  98.5 0.0 copy-done.2
  98.5 0.2 select_reduce_fusion.2
  98.7 1.8 %subtract_divide_fusion = f32[32,2048]{1,0:T(8,128)} fusion(f32[32,2048]{1,0:T(8,128)} %shard_map.78, f32[2048]{0:T(1024)S(1)} %get-tuple-element.3, f32[2048]{0:T(1024)S(1)} %get-tuple-element.2, f32[32]{0:T(128)S(1)} %add.8), kind=kLoop, calls=%fused_computation.4 | loop fusion | flops 196608 | bytes 540800 | tf_op jit(solution)/shard_map/div | solution.py:219
  100.5 1.7 %copy.9 = f32[32,2048]{1,0:T(8,128)} copy(f32[32,2048]{1,0:T(8,128)} %shard_map.78) | data formatting | bytes 524288
  (3 shorter events, 0.0 us)
Async XLA Ops:
  50.6 43.9 %copy-start = (s32[2048,2]{0,1:T(2,128)S(1)}, s32[2048,2]{0,1:T(2,128)}, u32[]{:S(2)}) copy-start(s32[2048,2]{0,1:T(2,128)} %param.9) | copy-start | bytes 49156
  50.6 44.0 %copy-start.3 = (f32[1536]{0:T(1024)S(1)}, f32[1536]{0:T(1024)}, u32[]{:S(2)}) copy-start(f32[1536]{0:T(1024)} %param.11) | copy-start | bytes 18436
  50.6 47.9 %copy-start.1 = (s32[32,2]{0,1:T(2,128)S(1)}, s32[32,2]{0,1:T(2,128)}, u32[]{:S(2)}) copy-start(s32[32,2]{0,1:T(2,128)} %param.8) | copy-start | bytes 772
  50.6 47.9 %copy-start.2 = (f32[128]{0:T(128)S(1)}, f32[128]{0:T(128)}, u32[]{:S(2)}) copy-start(f32[128]{0:T(128)} %param.10) | copy-start | bytes 1540

commit v3 on v2

--- a/solution.py
+++ b/solution.py
@@ -21,7 +21,7 @@
         row_block,
         col_block,
         (((1,), (1,)), ((), ())),
-        precision=lax.Precision.HIGHEST,
+        precision=lax.Precision.HIGH,
         preferred_element_type=jnp.float32,
     )
 
@@ -211,10 +211,10 @@
 def on_device(n_ab, n_cd, amplitudes, integrals, ij_pairs, ab_pairs, eps_occ, eps_vir):
     partial_value = contract_rows(gather_rows(amplitudes, n_ab), integrals)
     ladder = scatter_rows(partial_value, n_cd)
-    first_occ = lookup_energy(ij_pairs[:, 0], eps_occ)[:, None]
-    second_occ = lookup_energy(ij_pairs[:, 1], eps_occ)[:, None]
-    first_vir = lookup_energy(ab_pairs[:, 0], eps_vir)[None, :]
-    second_vir = lookup_energy(ab_pairs[:, 1], eps_vir)[None, :]
+    first_occ = eps_occ[ij_pairs[:, 0]][:, None]
+    second_occ = eps_occ[ij_pairs[:, 1]][:, None]
+    first_vir = eps_vir[ab_pairs[:, 0]][None, :]
+    second_vir = eps_vir[ab_pairs[:, 1]][None, :]
     denominator = first_occ + second_occ - first_vir - second_vir
     update = ladder / denominator
     return (ladder, update)

time: 102 us -> 119 us (1.17)
  local copies, waits for them, and re-layouts: 1.71 us -> 25.7 us
  other arithmetic: 5.87 us -> 0.87 us
  matrix products: 10.4 us -> 7.99 us
    gather x0 -> x4, local copies, waits for them, and re-layouts: none -> 25 us  [the longest x1 11.8 us: on_device(): second_vir = eps_vir[ab_pairs[:, 1]][None, :]]
    reduce_sum x2 -> x0, other arithmetic: 4.09 us -> none  [lookup_energy(): return jnp.sum(picked, axis=1)]
    dot_general x1, matrix products: 10.4 us -> 7.99 us  [contract_rows(): lax.dot_general(row_block, col_block, (((1,), (1,)), ((), ())), precision...]
where the time goes in v3:
time: 119 us
  Pallas kernels  83.7 us (70%)
  local copies, waits for them, and re-layouts  25.7 us (22%)
  matrix products  7.99 us (7%)
    pallas_call x1, Pallas kernels, scatter_rows(): pl.pallas_call(functools.partial(scatter_kernel, n_y), out_shape=jax.Shap...  44 us
    pallas_call x1, Pallas kernels, gather_rows(): pl.pallas_call(functools.partial(gather_kernel, n), out_shape=jax.ShapeDt...  39.7 us
    gather x1, local copies, waits for them, and re-layouts, on_device(): second_vir = eps_vir[ab_pairs[:, 1]][None, :]  11.8 us
    gather x1, local copies, waits for them, and re-layouts, on_device(): first_vir = eps_vir[ab_pairs[:, 0]][None, :]  11.8 us
    dot_general x1, matrix products, contract_rows(): lax.dot_general(row_block, col_block, (((1,), (1,)), ((), ())), precision...  7.99 us

profile of v3, /device:TPU:6, one launch (start us, length us, event | category | flops | bytes accessed | tf_op | source)
XLA Modules:
  0.0 119.0 jit_solution(3187043717560114111)
XLA Ops:
  0.6 0.0 copy-start
  0.6 39.7 %shard_map.77 = f32[512,512]{1,0:T(8,128)} custom-call(f32[16,512]{1,0:T(8,128)} %amp_ref.1), custom_call_target="tpu_custom_call" | custom-call | tf_op jit(solution)/shard_map/pallas_call | solution.py:85
  40.3 8.0 %fusion.2 = f32[512,2048]{1,0:T(8,128)} fusion(f32[512,512]{1,0:T(8,128)} %shard_map.77, f32[2048,512]{1,0:T(8,128)} %param.7), kind=kOutput, calls=%fused_computation.15 | convolution fusion | flops 3221225472 | bytes 9437184 | tf_op jit(solution)/shard_map/dot_general | solution.py:20
  48.3 0.0 copy-start.3
  48.3 44.0 %shard_map.78 = f32[32,2048]{1,0:T(8,128)} custom-call(f32[8,2,32,2048]{3,2,1,0:T(8,128)} %bitcast.9), custom_call_target="tpu_custom_call" | custom-call | tf_op jit(solution)/shard_map/pallas_call | solution.py:191
  92.3 0.0 copy-done.3
  92.4 0.0 copy-done
  92.4 11.8 %gather_fusion.3 = f32[2048]{0:T(1024)S(1)} fusion(f32[1536]{0:T(1024)S(1)} %copy-done, s32[2048]{0:T(1024)S(1)} %broadcast_clamp_fusion), kind=kCustom, calls=%fused_computation.3 | custom fusion | bytes 24576 | tf_op jit(solution)/shard_map/gather | solution.py:217
  104.2 0.0 copy-start.4
  104.2 0.0 copy-start.1
  104.2 0.0 copy-start.2
  104.2 11.8 %gather_fusion.2 = f32[2048]{0:T(1024)S(1)} fusion(f32[1536]{0:T(1024)S(1)} %copy-done, s32[2048]{0:T(1024)S(1)} %broadcast_clamp_fusion.1), kind=kCustom, calls=%fused_computation.2 | custom fusion | bytes 24576 | tf_op jit(solution)/shard_map/gather | solution.py:216
  116.0 0.0 copy-done.4
  116.0 0.0 copy-done.1
  116.1 0.7 gather_fusion
  116.7 0.7 gather_fusion.1
  117.5 0.0 copy-done.2
  117.5 0.8 subtract_divide_fusion
  118.3 0.7 copy.9
  (6 shorter events, 0.1 us)
Async XLA Ops:
  0.6 91.7 %copy-start = (f32[1536]{0:T(1024)S(1)}, f32[1536]{0:T(1024)}, u32[]{:S(2)}) copy-start(f32[1536]{0:T(1024)} %param.11) | copy-start | bytes 18436
  48.3 44.0 %copy-start.3 = (s32[2048,2]{0,1:T(2,128)S(1)}, s32[2048,2]{0,1:T(2,128)}, u32[]{:S(2)}) copy-start(s32[2048,2]{0,1:T(2,128)} %param.9) | copy-start | bytes 49156
  104.2 11.8 %copy-start.4 = (s32[32,2]{0,1:T(2,128)S(1)}, s32[32,2]{0,1:T(2,128)}, u32[]{:S(2)}) copy-start(s32[32,2]{0,1:T(2,128)} %param.8) | copy-start | bytes 772
  104.2 11.9 %copy-start.1 = (f32[128]{0:T(128)S(1)}, f32[128]{0:T(128)}, u32[]{:S(2)}) copy-start(f32[128]{0:T(128)} %param.10) | copy-start | bytes 1540
  104.2 13.3 %copy-start.2 = (f32[32,2048]{1,0:T(8,128)S(1)}, f32[32,2048]{1,0:T(8,128)}, u32[]{:S(2)}) copy-start(f32[32,2048]{1,0:T(8,128)} %shard_map.78) | copy-start | bytes 786436

commit v4 on v2

--- a/solution.py
+++ b/solution.py
@@ -11,9 +11,18 @@
 
 
 def lookup_energy(indices, energies):
-    positions = lax.broadcasted_iota(jnp.int32, (indices.shape[0], energies.shape[0]), 1)
-    picked = jnp.where(indices[:, None] == positions, energies[None, :], jnp.float32(0.0))
-    return jnp.sum(picked, axis=1)
+    lanes = 128
+    groups = -(-energies.shape[0] // lanes)
+    table = jnp.pad(energies, (0, groups * lanes - energies.shape[0])).reshape(groups, lanes)
+    low = lax.rem(indices, lanes)
+    high = indices // lanes
+    one_hot = (low[:, None] == lax.broadcasted_iota(jnp.int32, (indices.shape[0], lanes), 1)).astype(jnp.float32)
+    by_group = lax.dot_general(
+        one_hot, table, (((1,), (1,)), ((), ())),
+        precision=lax.Precision.HIGHEST, preferred_element_type=jnp.float32,
+    )
+    chosen = high[:, None] == lax.broadcasted_iota(jnp.int32, by_group.shape, 1)
+    return jnp.sum(jnp.where(chosen, by_group, jnp.float32(0.0)), axis=1)
 
 
 def contract_rows(row_block, col_block):
@@ -21,7 +30,7 @@
         row_block,
         col_block,
         (((1,), (1,)), ((), ())),
-        precision=lax.Precision.HIGHEST,
+        precision=lax.Precision.HIGH,
         preferred_element_type=jnp.float32,
     )
 

time: 102 us -> 98.2 us (0.963)
  other arithmetic: 5.87 us -> 1.88 us
    reduce_sum x2 -> x0, other arithmetic: 4.09 us -> none  [lookup_energy(): return jnp.sum(picked, axis=1)]
    dot_general x1, matrix products: 10.4 us -> 7.98 us  [contract_rows(): lax.dot_general(row_block, col_block, (((1,), (1,)), ((), ())), precision...]
    dot_general x0 -> x4, matrix products: none -> 1.86 us  [lookup_energy(): lax.dot_general(one_hot, table, (((1,), (1,)), ((), ())), precision=lax.P...]
where the time goes in v4:
time: 98.2 us; the launch traced here: 97.8 us
  Pallas kernels  83.7 us (85%)
  matrix products  9.85 us (10%)
  other arithmetic  1.88 us (2%)
  local copies, waits for them, and re-layouts  1.69 us (2%)
    pallas_call x1, Pallas kernels, scatter_rows(): pl.pallas_call(functools.partial(scatter_kernel, n_y), out_shape=jax.Shap...  44 us
    pallas_call x1, Pallas kernels, gather_rows(): pl.pallas_call(functools.partial(gather_kernel, n), out_shape=jax.ShapeDt...  39.7 us
    dot_general x1, matrix products, contract_rows(): lax.dot_general(row_block, col_block, (((1,), (1,)), ((), ())), precision...  7.98 us

profile of v4, /device:TPU:6, one launch (start us, length us, event | category | flops | bytes accessed | tf_op | source)
XLA Modules:
  0.0 97.8 jit_solution(9778123332080758322)
XLA Ops:
  0.6 0.0 copy-start
  0.6 39.7 %shard_map.77 = f32[512,512]{1,0:T(8,128)} custom-call(f32[16,512]{1,0:T(8,128)} %amp_ref.1), custom_call_target="tpu_custom_call" | custom-call | tf_op jit(solution)/shard_map/pallas_call | solution.py:94
  40.3 8.0 %fusion.17 = f32[512,2048]{1,0:T(8,128)} fusion(f32[512,512]{1,0:T(8,128)} %shard_map.77, f32[2048,512]{1,0:T(8,128)} %param.7), kind=kOutput, calls=%fused_computation.50 | convolution fusion | flops 3221225472 | bytes 9437184 | tf_op jit(solution)/shard_map/dot_general | solution.py:29
  48.3 0.0 copy-start.1
  48.3 0.0 copy-start.2
  48.3 0.0 copy-start.3
  48.3 44.0 %shard_map.78 = f32[32,2048]{1,0:T(8,128)} custom-call(f32[8,2,32,2048]{3,2,1,0:T(8,128)} %bitcast.50), custom_call_target="tpu_custom_call" | custom-call | tf_op jit(solution)/shard_map/pallas_call | solution.py:200
  92.3 0.0 copy-done.1
  92.3 0.1 and_select_fusion.1
  92.4 0.0 copy-done
  92.4 0.7 fusion.1
  93.2 0.7 fusion
  93.9 0.0 copy-done.2
  94.0 0.0 copy-done.3
  94.0 0.2 fusion.2
  94.2 0.2 fusion.4
  94.4 1.8 %subtract_divide_fusion = f32[32,2048]{1,0:T(8,128)} fusion(f32[32,2048]{1,0:T(8,128)} %shard_map.78, f32[2048]{0:T(1024)S(1)} %fusion.1, f32[2048]{0:T(1024)S(1)} %fusion, f32[32]{0:T(128)S(1)} %fusion.4), kind=kLoop, calls=%fused_computation.13 | loop fusion | flops 196608 | bytes 540800 | tf_op jit(solution)/shard_map/div | solution.py:228
  96.2 1.7 %copy.9 = f32[32,2048]{1,0:T(8,128)} copy(f32[32,2048]{1,0:T(8,128)} %shard_map.78) | data formatting | bytes 524288
  (1 shorter events, 0.0 us)
Async XLA Ops:
  0.6 91.8 %copy-start = (f32[1536]{0:T(1024)S(1)}, f32[1536]{0:T(1024)}, u32[]{:S(2)}) copy-start(f32[1536]{0:T(1024)} %param.11) | copy-start | bytes 18436
  48.3 44.0 %copy-start.1 = (s32[2048,2]{0,1:T(2,128)S(1)}, s32[2048,2]{0,1:T(2,128)}, u32[]{:S(2)}) copy-start(s32[2048,2]{0,1:T(2,128)} %param.9) | copy-start | bytes 49156
  48.3 45.6 %copy-start.2 = (s32[32,2]{0,1:T(2,128)S(1)}, s32[32,2]{0,1:T(2,128)}, u32[]{:S(2)}) copy-start(s32[32,2]{0,1:T(2,128)} %param.8) | copy-start | bytes 772
  48.3 45.6 %copy-start.3 = (f32[128]{0:T(128)S(1)}, f32[128]{0:T(128)}, u32[]{:S(2)}) copy-start(f32[128]{0:T(128)} %param.10) | copy-start | bytes 1540

commit v5 on v4

--- a/solution.py
+++ b/solution.py
@@ -105,7 +105,7 @@
     )(amplitudes)
 
 
-def scatter_kernel(n_y, part_ref, out_ref, pair, send_r, recv_r, send_l, recv_l,
+def scatter_kernel(n_y, n_chunks, part_ref, out_ref, pair, send_r, recv_r, send_l, recv_l,
                    pair_send, pair_recv, ring_send, ring_recv):
     ab = lax.axis_index("ab")
     cd = lax.axis_index("cd")
@@ -115,6 +115,7 @@
     left = lax.rem(y + n_y - 1, n_y) * 2 + core
     partner = y * 2 + other
     half = out_ref.shape[1] // 2
+    width = half // n_chunks
 
     barrier = pltpu.get_barrier_semaphore()
     for peer in (partner, right, left):
@@ -145,15 +146,19 @@
         b = lax.rem(y + k + n_y, n_y)
         return part_ref[b, core, :, cols] + pair[b, :, cols]
 
-    lo, hi = slice(0, half), slice(half, 2 * half)
-
-    def ring_copy(d, s):
-        src, dst = (send_r, recv_r) if d == 0 else (send_l, recv_l)
-        return pltpu.make_async_remote_copy(
-            src_ref=src.at[s],
-            dst_ref=dst.at[s],
-            send_sem=ring_send.at[d, s],
-            recv_sem=ring_recv.at[d, s],
+    def columns(d, q):
+        start = d * half + q * width
+        return slice(start, start + width)
+
+    sends = (send_r, send_l)
+    recvs = (recv_r, recv_l)
+
+    def ring_copy(d, s, q):
+        return pltpu.make_async_remote_copy(
+            src_ref=sends[d].at[s, q],
+            dst_ref=recvs[d].at[s, q],
+            send_sem=ring_send.at[d, s, q],
+            recv_sem=ring_recv.at[d, s, q],
             device_id=(ab, right if d == 0 else left),
             device_id_type=MESH,
         )
@@ -169,49 +174,50 @@
     for s in range(n_y - 1):
         need(-(s + 1))
         need(s + 1)
-        if s == 0:
-            send_r[s] = own(-1, lo)
-            send_l[s] = own(1, hi)
-        else:
-            ring_copy(0, s - 1).wait_recv()
-            send_r[s] = recv_r[s - 1] + own(-(s + 1), lo)
-            ring_copy(1, s - 1).wait_recv()
-            send_l[s] = recv_l[s - 1] + own(s + 1, hi)
-        ring_copy(0, s).start()
-        ring_copy(1, s).start()
+        for q in range(n_chunks):
+            for d in (0, 1):
+                k = -(s + 1) if d == 0 else s + 1
+                if s == 0:
+                    sends[d][s, q] = own(k, columns(d, q))
+                else:
+                    ring_copy(d, s - 1, q).wait_recv()
+                    sends[d][s, q] = recvs[d][s - 1, q] + own(k, columns(d, q))
+                ring_copy(d, s, q).start()
     need(0)
-    ring_copy(0, n_y - 2).wait_recv()
-    out_ref[:, lo] = recv_r[n_y - 2] + own(0, lo)
-    ring_copy(1, n_y - 2).wait_recv()
-    out_ref[:, hi] = recv_l[n_y - 2] + own(0, hi)
+    for q in range(n_chunks):
+        for d in (0, 1):
+            ring_copy(d, n_y - 2, q).wait_recv()
+            out_ref[:, columns(d, q)] = recvs[d][n_y - 2, q] + own(0, columns(d, q))
     for k in order:
         pair_copy(k).wait_send()
     for s in range(n_y - 1):
-        ring_copy(0, s).wait_send()
-        ring_copy(1, s).wait_send()
-
-
-def scatter_rows(partial_value, n_cd):
+        for q in range(n_chunks):
+            ring_copy(0, s, q).wait_send()
+            ring_copy(1, s, q).wait_send()
+
+
+def scatter_rows(partial_value, n_cd, n_chunks=4):
     n_y = n_cd // 2
     total_rows, cols = partial_value.shape
     rows = total_rows // n_cd
     blocks = partial_value.reshape(n_y, 2, rows, cols)
-    half = cols // 2
+    width = cols // 2 // n_chunks
+    slots = pltpu.VMEM((n_y - 1, n_chunks, rows, width), jnp.float32)
     return pl.pallas_call(
-        functools.partial(scatter_kernel, n_y),
+        functools.partial(scatter_kernel, n_y, n_chunks),
         out_shape=jax.ShapeDtypeStruct((rows, cols), partial_value.dtype),
         in_specs=[pl.BlockSpec(memory_space=pltpu.VMEM)],
         out_specs=pl.BlockSpec(memory_space=pltpu.VMEM),
         scratch_shapes=[
             pltpu.VMEM((n_y, rows, cols), jnp.float32),
-            pltpu.VMEM((n_y - 1, rows, half), jnp.float32),
-            pltpu.VMEM((n_y - 1, rows, half), jnp.float32),
-            pltpu.VMEM((n_y - 1, rows, half), jnp.float32),
-            pltpu.VMEM((n_y - 1, rows, half), jnp.float32),
+            slots,
+            slots,
+            slots,
+            slots,
             pltpu.SemaphoreType.DMA((n_y,)),
             pltpu.SemaphoreType.DMA((n_y,)),
-            pltpu.SemaphoreType.DMA((2, n_y - 1)),
-            pltpu.SemaphoreType.DMA((2, n_y - 1)),
+            pltpu.SemaphoreType.DMA((2, n_y - 1, n_chunks)),
+            pltpu.SemaphoreType.DMA((2, n_y - 1, n_chunks)),
         ],
         compiler_params=pltpu.CompilerParams(collective_id=1, has_side_effects=True),
     )(blocks)

time: 98.2 us -> 88.9 us (0.905)
  the two profiles are of different devices: /device:TPU:6 before, /device:TPU:1 now
where the time goes in v5:
time: 88.9 us; the launch traced here: 87.1 us
  Pallas kernels  72.9 us (82%)
  matrix products  9.85 us (11%)
  other arithmetic  1.88 us (2%)
  local copies, waits for them, and re-layouts  1.69 us (2%)
    pallas_call x1, Pallas kernels, gather_rows(): pl.pallas_call(functools.partial(gather_kernel, n), out_shape=jax.ShapeDt...  37 us
    pallas_call x1, Pallas kernels, scatter_rows(): pl.pallas_call(functools.partial(scatter_kernel, n_y, n_chunks), out_shap...  35.9 us
    dot_general x1, matrix products, contract_rows(): lax.dot_general(row_block, col_block, (((1,), (1,)), ((), ())), precision...  7.98 us
    dot_general x4, matrix products, lookup_energy(): lax.dot_general(one_hot, table, (((1,), (1,)), ((), ())), precision=lax.P...  1.86 us
    div x1, other arithmetic, on_device(): update = ladder / denominator  1.79 us

profile of v5, /device:TPU:1, one launch (start us, length us, event | category | flops | bytes accessed | tf_op | source)
XLA Modules:
  0.0 87.1 jit_solution(13836295027679052883)
XLA Ops:
  0.6 0.0 copy-start
  0.6 37.0 %shard_map.77 = f32[512,512]{1,0:T(8,128)} custom-call(f32[16,512]{1,0:T(8,128)} %amp_ref.1), custom_call_target="tpu_custom_call" | custom-call | tf_op jit(solution)/shard_map/pallas_call | solution.py:94
  37.7 8.0 %fusion.17 = f32[512,2048]{1,0:T(8,128)} fusion(f32[512,512]{1,0:T(8,128)} %shard_map.77, f32[2048,512]{1,0:T(8,128)} %param.7), kind=kOutput, calls=%fused_computation.50 | convolution fusion | flops 3221225472 | bytes 9437184 | tf_op jit(solution)/shard_map/dot_general | solution.py:29
  45.7 0.0 copy-start.1
  45.7 0.0 copy-start.2
  45.7 0.0 copy-start.3
  45.7 35.9 %shard_map.78 = f32[32,2048]{1,0:T(8,128)} custom-call(f32[8,2,32,2048]{3,2,1,0:T(8,128)} %bitcast.50), custom_call_target="tpu_custom_call" | custom-call | tf_op jit(solution)/shard_map/pallas_call | solution.py:206
  81.6 0.0 copy-done.1
  81.6 0.1 and_select_fusion.1
  81.7 0.0 copy-done
  81.7 0.7 fusion.1
  82.4 0.7 fusion
  83.2 0.0 copy-done.2
  83.2 0.0 copy-done.3
  83.2 0.2 fusion.2
  83.4 0.2 fusion.4
  83.6 1.8 %subtract_divide_fusion = f32[32,2048]{1,0:T(8,128)} fusion(f32[32,2048]{1,0:T(8,128)} %shard_map.78, f32[2048]{0:T(1024)S(1)} %fusion.1, f32[2048]{0:T(1024)S(1)} %fusion, f32[32]{0:T(128)S(1)} %fusion.4), kind=kLoop, calls=%fused_computation.13 | loop fusion | flops 196608 | bytes 540800 | tf_op jit(solution)/shard_map/div | solution.py:234
  85.4 1.7 %copy.9 = f32[32,2048]{1,0:T(8,128)} copy(f32[32,2048]{1,0:T(8,128)} %shard_map.78) | data formatting | bytes 524288
  (1 shorter events, 0.0 us)
Async XLA Ops:
  0.6 81.1 %copy-start = (f32[1536]{0:T(1024)S(1)}, f32[1536]{0:T(1024)}, u32[]{:S(2)}) copy-start(f32[1536]{0:T(1024)} %param.11) | copy-start | bytes 18436
  45.7 35.9 %copy-start.1 = (s32[2048,2]{0,1:T(2,128)S(1)}, s32[2048,2]{0,1:T(2,128)}, u32[]{:S(2)}) copy-start(s32[2048,2]{0,1:T(2,128)} %param.9) | copy-start | bytes 49156
  45.7 37.5 %copy-start.2 = (s32[32,2]{0,1:T(2,128)S(1)}, s32[32,2]{0,1:T(2,128)}, u32[]{:S(2)}) copy-start(s32[32,2]{0,1:T(2,128)} %param.8) | copy-start | bytes 772
  45.7 37.6 %copy-start.3 = (f32[128]{0:T(128)S(1)}, f32[128]{0:T(128)}, u32[]{:S(2)}) copy-start(f32[128]{0:T(128)} %param.10) | copy-start | bytes 1540

commit v6 on v5

--- a/solution.py
+++ b/solution.py
@@ -35,74 +35,122 @@
     )
 
 
-def gather_kernel(n, amp_ref, out_ref, held, send_sems, recv_sems):
-    me = lax.axis_index("ab")
+def gather_kernel(n_x, n_z, amp_ref, out_ref, held, local_sem, x_send, x_recv, z_send, z_recv):
+    ab = lax.axis_index("ab")
     cd = lax.axis_index("cd")
+    z, x = ab // n_x, lax.rem(ab, n_x)
     rows = amp_ref.shape[0]
+    group = rows * n_x
+    cols = amp_ref.shape[1]
+    up = lax.rem(z + 1, n_z) * n_x + x
+    down = lax.rem(z + n_z - 1, n_z) * n_x + x
 
     barrier = pltpu.get_barrier_semaphore()
-
-    def greet(i, carry):
-        peer = lax.rem(me + i, n)
-        pl.semaphore_signal(barrier, inc=1, device_id=(peer, cd), device_id_type=MESH)
-        return carry
-
-    lax.fori_loop(1, n, greet, 0)
-    pl.semaphore_wait(barrier, n - 1)
-
-    mine = pl.ds(pl.multiple_of(me * rows, rows), rows)
-
-    def copy_to(peer):
+    for i in range(1, n_x):
+        pl.semaphore_signal(barrier, inc=1, device_id=(z * n_x + lax.rem(x + i, n_x), cd), device_id_type=MESH)
+    pl.semaphore_signal(barrier, inc=1, device_id=(up, cd), device_id_type=MESH)
+    pl.semaphore_signal(barrier, inc=1, device_id=(down, cd), device_id_type=MESH)
+    pl.semaphore_wait(barrier, n_x + 1)
+
+    def block_rows(a_index):
+        return pl.ds(pl.multiple_of(a_index * rows, rows), rows)
+
+    def x_copy(i, receiving):
+        sender = lax.rem(x + n_x - i, n_x) if receiving else x
+        target = lax.rem(x + i, n_x)
         return pltpu.make_async_remote_copy(
             src_ref=amp_ref,
-            dst_ref=held.at[mine],
-            send_sem=send_sems.at[peer],
-            recv_sem=recv_sems.at[me],
-            device_id=(peer, cd),
-            device_id_type=MESH,
-        )
-
-    def copy_from(peer):
-        theirs = pl.ds(pl.multiple_of(peer * rows, rows), rows)
-        return pltpu.make_async_remote_copy(
-            src_ref=amp_ref,
-            dst_ref=held.at[theirs],
-            send_sem=send_sems.at[peer],
-            recv_sem=recv_sems.at[peer],
-            device_id=(peer, cd),
-            device_id_type=MESH,
-        )
-
-    def send(i, carry):
-        copy_to(lax.rem(me + i, n)).start()
-        return carry
-
-    lax.fori_loop(1, n, send, 0)
-    held[mine, :] = amp_ref[...]
-
-    def finish(i, carry):
-        copy_to(lax.rem(me + i, n)).wait_send()
-        copy_from(lax.rem(me + n - i, n)).wait_recv()
-        return carry
-
-    lax.fori_loop(1, n, finish, 0)
+            dst_ref=held.at[block_rows(z * n_x + sender)],
+            send_sem=x_send.at[target],
+            recv_sem=x_recv.at[sender],
+            device_id=(z * n_x + target, cd),
+            device_id_type=MESH,
+        )
+
+    for i in range(1, n_x):
+        x_copy(i, False).start()
+    local = pltpu.make_async_copy(amp_ref, held.at[block_rows(ab)], local_sem)
+    local.start()
+    local.wait()
+    for i in range(1, n_x):
+        x_copy(i, True).wait_recv()
+
+    steps = n_z // 2
+
+    def z_copy(d, t, q):
+        source_z = lax.rem(z + n_z - t, n_z) if d == 0 else lax.rem(z + t, n_z)
+        cols_here = slice(0, cols)
+        if t == steps - 1:
+            cols_here = slice(0, cols // 2) if d == 0 else slice(cols // 2, cols)
+        src = held.at[block_rows(source_z * n_x + q), cols_here]
+        return pltpu.make_async_remote_copy(
+            src_ref=src,
+            dst_ref=src,
+            send_sem=z_send.at[d, t, q],
+            recv_sem=z_recv.at[d, t, q],
+            device_id=(up if d == 0 else down, cd),
+            device_id_type=MESH,
+        )
+
+    def z_arrival(d, t, q):
+        source_z = lax.rem(z + n_z - t - 1, n_z) if d == 0 else lax.rem(z + t + 1, n_z)
+        cols_here = slice(0, cols)
+        if t == steps - 1:
+            cols_here = slice(0, cols // 2) if d == 0 else slice(cols // 2, cols)
+        dst = held.at[block_rows(source_z * n_x + q), cols_here]
+        return pltpu.make_async_remote_copy(
+            src_ref=dst,
+            dst_ref=dst,
+            send_sem=z_send.at[d, t, q],
+            recv_sem=z_recv.at[d, t, q],
+            device_id=(up if d == 0 else down, cd),
+            device_id_type=MESH,
+        )
+
+    for t in range(steps):
+        for q in range(n_x):
+            for d in (0, 1):
+                if t > 0:
+                    z_arrival(d, t - 1, q).wait_recv()
+                z_copy(d, t, q).start()
+    for q in range(n_x):
+        for d in (0, 1):
+            z_arrival(d, steps - 1, q).wait_recv()
+    for i in range(1, n_x):
+        x_copy(i, False).wait_send()
+    for t in range(steps):
+        for q in range(n_x):
+            for d in (0, 1):
+                z_copy(d, t, q).wait_send()
     out_ref[...] = held[...]
 
 
-def gather_rows(amplitudes, n):
+def gather_rows(amplitudes, n_x, n_z):
     rows, cols = amplitudes.shape
+    steps = n_z // 2
     return pl.pallas_call(
-        functools.partial(gather_kernel, n),
-        out_shape=jax.ShapeDtypeStruct((rows * n, cols), amplitudes.dtype),
+        functools.partial(gather_kernel, n_x, n_z),
+        out_shape=jax.ShapeDtypeStruct((rows * n_x * n_z, cols), amplitudes.dtype),
         in_specs=[pl.BlockSpec(memory_space=pltpu.VMEM)],
         out_specs=pl.BlockSpec(memory_space=pltpu.VMEM),
         scratch_shapes=[
-            pltpu.VMEM((rows * n, cols), amplitudes.dtype),
-            pltpu.SemaphoreType.DMA((n,)),
-            pltpu.SemaphoreType.DMA((n,)),
+            pltpu.VMEM((rows * n_x * n_z, cols), amplitudes.dtype),
+            pltpu.SemaphoreType.DMA(()),
+            pltpu.SemaphoreType.DMA((n_x,)),
+            pltpu.SemaphoreType.DMA((n_x,)),
+            pltpu.SemaphoreType.DMA((2, steps, n_x)),
+            pltpu.SemaphoreType.DMA((2, steps, n_x)),
         ],
         compiler_params=pltpu.CompilerParams(collective_id=0, has_side_effects=True),
     )(amplitudes)
+
+
+def x_extent(mesh):
+    first = mesh.devices.reshape(mesh.shape["ab"], -1)[:, 0]
+    try:
+        return len({d.coords[0] for d in first})
+    except AttributeError:
+        return 2
 
 
 def scatter_kernel(n_y, n_chunks, part_ref, out_ref, pair, send_r, recv_r, send_l, recv_l,
@@ -223,8 +271,8 @@
     )(blocks)
 
 
-def on_device(n_ab, n_cd, amplitudes, integrals, ij_pairs, ab_pairs, eps_occ, eps_vir):
-    partial_value = contract_rows(gather_rows(amplitudes, n_ab), integrals)
+def on_device(n_x, n_z, n_cd, amplitudes, integrals, ij_pairs, ab_pairs, eps_occ, eps_vir):
+    partial_value = contract_rows(gather_rows(amplitudes, n_x, n_z), integrals)
     ladder = scatter_rows(partial_value, n_cd)
     first_occ = lookup_energy(ij_pairs[:, 0], eps_occ)[:, None]
     second_occ = lookup_energy(ij_pairs[:, 1], eps_occ)[:, None]
@@ -239,7 +287,7 @@
     in_specs = (P("ab", "cd"), P("ab", "cd"), P("cd", None), P("ab", None), P(), P())
     out_specs = (P("cd", "ab"), P("cd", "ab"))
     return jax.shard_map(
-        functools.partial(on_device, mesh.shape["ab"], mesh.shape["cd"]),
+        functools.partial(on_device, x_extent(mesh), mesh.shape["ab"] // x_extent(mesh), mesh.shape["cd"]),
         mesh=mesh,
         in_specs=in_specs,
         out_specs=out_specs,

time: 88.9 us -> 81.5 us (0.917); the launches traced: 87.1 us -> 81.1 us
  Pallas kernels: 72.9 us -> 67 us
    pallas_call x1, Pallas kernels: 37 us -> 29.6 us  [gather_rows(): pl.pallas_call(functools.partial(gather_kernel, n_x, n_z), out_shape=jax....]
    pallas_call x1, Pallas kernels: 35.9 us -> 37.4 us  [scatter_rows(): pl.pallas_call(functools.partial(scatter_kernel, n_y, n_chunks), out_shap...]
where the time goes in v6:
time: 81.5 us; the launch traced here: 81.1 us
  Pallas kernels  67 us (82%)
  matrix products  9.85 us (12%)
  other arithmetic  1.88 us (2%)
  local copies, waits for them, and re-layouts  1.69 us (2%)
    pallas_call x1, Pallas kernels, scatter_rows(): pl.pallas_call(functools.partial(scatter_kernel, n_y, n_chunks), out_shap...  37.4 us
    pallas_call x1, Pallas kernels, gather_rows(): pl.pallas_call(functools.partial(gather_kernel, n_x, n_z), out_shape=jax....  29.6 us
    dot_general x1, matrix products, contract_rows(): lax.dot_general(row_block, col_block, (((1,), (1,)), ((), ())), precision...  7.98 us
    dot_general x4, matrix products, lookup_energy(): lax.dot_general(one_hot, table, (((1,), (1,)), ((), ())), precision=lax.P...  1.86 us
    div x1, other arithmetic, on_device(): update = ladder / denominator  1.79 us
    unnamed x9, local copies, waits for them, and re-layouts  1.69 us

profile of v6, /device:TPU:1, one launch (start us, length us, event | category | flops | bytes accessed | tf_op | source)
XLA Modules:
  0.0 81.1 jit_solution(3410475540462639468)
XLA Ops:
  0.6 0.0 copy-start
  0.6 29.6 %shard_map.77 = f32[512,512]{1,0:T(8,128)} custom-call(f32[16,512]{1,0:T(8,128)} %amp_ref.1), custom_call_target="tpu_custom_call" | custom-call | tf_op jit(solution)/shard_map/pallas_call | solution.py:131
  30.2 8.0 %fusion.17 = f32[512,2048]{1,0:T(8,128)} fusion(f32[512,512]{1,0:T(8,128)} %shard_map.77, f32[2048,512]{1,0:T(8,128)} %param.7), kind=kOutput, calls=%fused_computation.50 | convolution fusion | flops 3221225472 | bytes 9437184 | tf_op jit(solution)/shard_map/dot_general | solution.py:29
  38.2 0.0 copy-start.1
  38.2 0.0 copy-start.2
  38.2 0.0 copy-start.3
  38.2 37.4 %shard_map.78 = f32[32,2048]{1,0:T(8,128)} custom-call(f32[8,2,32,2048]{3,2,1,0:T(8,128)} %bitcast.50), custom_call_target="tpu_custom_call" | custom-call | tf_op jit(solution)/shard_map/pallas_call | solution.py:254
  75.6 0.0 copy-done.1
  75.6 0.1 and_select_fusion.1
  75.7 0.0 copy-done
  75.7 0.7 fusion.1
  76.5 0.7 fusion
  77.2 0.0 copy-done.2
  77.2 0.0 copy-done.3
  77.2 0.2 fusion.2
  77.4 0.2 fusion.4
  77.6 1.8 %subtract_divide_fusion = f32[32,2048]{1,0:T(8,128)} fusion(f32[32,2048]{1,0:T(8,128)} %shard_map.78, f32[2048]{0:T(1024)S(1)} %fusion.1, f32[2048]{0:T(1024)S(1)} %fusion, f32[32]{0:T(128)S(1)} %fusion.4), kind=kLoop, calls=%fused_computation.13 | loop fusion | flops 196608 | bytes 540800 | tf_op jit(solution)/shard_map/div | solution.py:282
  79.4 1.7 %copy.9 = f32[32,2048]{1,0:T(8,128)} copy(f32[32,2048]{1,0:T(8,128)} %shard_map.78) | data formatting | bytes 524288
  (1 shorter events, 0.0 us)
Async XLA Ops:
  0.6 75.1 %copy-start = (f32[1536]{0:T(1024)S(1)}, f32[1536]{0:T(1024)}, u32[]{:S(2)}) copy-start(f32[1536]{0:T(1024)} %param.11) | copy-start | bytes 18436
  38.2 37.4 %copy-start.1 = (s32[2048,2]{0,1:T(2,128)S(1)}, s32[2048,2]{0,1:T(2,128)}, u32[]{:S(2)}) copy-start(s32[2048,2]{0,1:T(2,128)} %param.9) | copy-start | bytes 49156
  38.2 39.0 %copy-start.2 = (s32[32,2]{0,1:T(2,128)S(1)}, s32[32,2]{0,1:T(2,128)}, u32[]{:S(2)}) copy-start(s32[32,2]{0,1:T(2,128)} %param.8) | copy-start | bytes 772
  38.2 39.0 %copy-start.3 = (f32[128]{0:T(128)S(1)}, f32[128]{0:T(128)}, u32[]{:S(2)}) copy-start(f32[128]{0:T(128)} %param.10) | copy-start | bytes 1540

commit v7 on v6

--- a/solution.py
+++ b/solution.py
@@ -244,7 +244,7 @@
             ring_copy(1, s, q).wait_send()
 
 
-def scatter_rows(partial_value, n_cd, n_chunks=4):
+def scatter_rows(partial_value, n_cd, n_chunks=8):
     n_y = n_cd // 2
     total_rows, cols = partial_value.shape
     rows = total_rows // n_cd

time: 81.5 us -> 81.8 us (level)
  no operation moved by 1% of the time
where the time goes in v7:
time: 81.8 us; the launch traced here: 80.9 us
  Pallas kernels  66.8 us (82%)
  matrix products  9.85 us (12%)
  other arithmetic  1.88 us (2%)
  local copies, waits for them, and re-layouts  1.69 us (2%)
    pallas_call x1, Pallas kernels, scatter_rows(): pl.pallas_call(functools.partial(scatter_kernel, n_y, n_chunks), out_shap...  37.2 us
    pallas_call x1, Pallas kernels, gather_rows(): pl.pallas_call(functools.partial(gather_kernel, n_x, n_z), out_shape=jax....  29.6 us
    dot_general x1, matrix products, contract_rows(): lax.dot_general(row_block, col_block, (((1,), (1,)), ((), ())), precision...  7.98 us
    dot_general x4, matrix products, lookup_energy(): lax.dot_general(one_hot, table, (((1,), (1,)), ((), ())), precision=lax.P...  1.86 us
    div x1, other arithmetic, on_device(): update = ladder / denominator  1.79 us
    unnamed x9, local copies, waits for them, and re-layouts  1.69 us

profile of v7, /device:TPU:1, one launch (start us, length us, event | category | flops | bytes accessed | tf_op | source)
XLA Modules:
  0.0 80.9 jit_solution(9392234617574490437)
XLA Ops:
  0.6 0.0 copy-start
  0.6 29.6 %shard_map.77 = f32[512,512]{1,0:T(8,128)} custom-call(f32[16,512]{1,0:T(8,128)} %amp_ref.1), custom_call_target="tpu_custom_call" | custom-call | tf_op jit(solution)/shard_map/pallas_call | solution.py:131
  30.2 8.0 %fusion.17 = f32[512,2048]{1,0:T(8,128)} fusion(f32[512,512]{1,0:T(8,128)} %shard_map.77, f32[2048,512]{1,0:T(8,128)} %param.7), kind=kOutput, calls=%fused_computation.50 | convolution fusion | flops 3221225472 | bytes 9437184 | tf_op jit(solution)/shard_map/dot_general | solution.py:29
  38.2 0.0 copy-start.1
  38.2 0.0 copy-start.2
  38.2 0.0 copy-start.3
  38.2 37.2 %shard_map.78 = f32[32,2048]{1,0:T(8,128)} custom-call(f32[8,2,32,2048]{3,2,1,0:T(8,128)} %bitcast.50), custom_call_target="tpu_custom_call" | custom-call | tf_op jit(solution)/shard_map/pallas_call | solution.py:254
  75.4 0.0 copy-done.1
  75.4 0.1 and_select_fusion.1
  75.5 0.0 copy-done
  75.5 0.7 fusion.1
  76.3 0.7 fusion
  77.0 0.0 copy-done.2
  77.0 0.0 copy-done.3
  77.0 0.2 fusion.2
  77.2 0.2 fusion.4
  77.4 1.8 %subtract_divide_fusion = f32[32,2048]{1,0:T(8,128)} fusion(f32[32,2048]{1,0:T(8,128)} %shard_map.78, f32[2048]{0:T(1024)S(1)} %fusion.1, f32[2048]{0:T(1024)S(1)} %fusion, f32[32]{0:T(128)S(1)} %fusion.4), kind=kLoop, calls=%fused_computation.13 | loop fusion | flops 196608 | bytes 540800 | tf_op jit(solution)/shard_map/div | solution.py:282
  79.2 1.7 %copy.9 = f32[32,2048]{1,0:T(8,128)} copy(f32[32,2048]{1,0:T(8,128)} %shard_map.78) | data formatting | bytes 524288
  (1 shorter events, 0.0 us)
Async XLA Ops:
  0.6 74.9 %copy-start = (f32[1536]{0:T(1024)S(1)}, f32[1536]{0:T(1024)}, u32[]{:S(2)}) copy-start(f32[1536]{0:T(1024)} %param.11) | copy-start | bytes 18436
  38.2 37.2 %copy-start.1 = (s32[2048,2]{0,1:T(2,128)S(1)}, s32[2048,2]{0,1:T(2,128)}, u32[]{:S(2)}) copy-start(s32[2048,2]{0,1:T(2,128)} %param.9) | copy-start | bytes 49156
  38.2 38.8 %copy-start.2 = (s32[32,2]{0,1:T(2,128)S(1)}, s32[32,2]{0,1:T(2,128)}, u32[]{:S(2)}) copy-start(s32[32,2]{0,1:T(2,128)} %param.8) | copy-start | bytes 772
  38.2 38.8 %copy-start.3 = (f32[128]{0:T(128)S(1)}, f32[128]{0:T(128)}, u32[]{:S(2)}) copy-start(f32[128]{0:T(128)} %param.10) | copy-start | bytes 1540

commit v8 on v6

--- a/solution.py
+++ b/solution.py
@@ -170,25 +170,22 @@
         pl.semaphore_signal(barrier, inc=1, device_id=(ab, peer), device_id_type=MESH)
     pl.semaphore_wait(barrier, 3)
 
-    order = []
-    for k in list(range(1, n_y // 2 + 1)) + [0]:
-        for sign in (1, -1):
-            if (sign * k) % n_y not in [j % n_y for j in order]:
-                order.append(sign * k)
-
-    def pair_copy(k):
-        b = lax.rem(y + k + n_y, n_y)
-        return pltpu.make_async_remote_copy(
-            src_ref=part_ref.at[b, other],
-            dst_ref=pair.at[b],
-            send_sem=pair_send.at[b],
-            recv_sem=pair_recv.at[b],
+    order = [item for s in range(n_y - 1) for item in ((-(s + 1), 0), (s + 1, 1))] + [(0, 0), (0, 1)]
+
+    def pair_copy(k, d):
+        b = lax.rem(y + k + n_y * n_y, n_y)
+        cols = slice(d * half, (d + 1) * half)
+        return pltpu.make_async_remote_copy(
+            src_ref=part_ref.at[b, other, :, cols],
+            dst_ref=pair.at[b, :, cols],
+            send_sem=pair_send.at[b, d],
+            recv_sem=pair_recv.at[b, d],
             device_id=(ab, partner),
             device_id_type=MESH,
         )
 
-    for k in order:
-        pair_copy(k).start()
+    for k, d in order:
+        pair_copy(k, d).start()
 
     def own(k, cols):
         b = lax.rem(y + k + n_y, n_y)
@@ -211,17 +208,9 @@
             device_id_type=MESH,
         )
 
-    waited = set()
-
-    def need(k):
-        k = k % n_y
-        if k not in waited:
-            waited.add(k)
-            pair_copy(k if k <= n_y // 2 else k - n_y).wait_recv()
-
     for s in range(n_y - 1):
-        need(-(s + 1))
-        need(s + 1)
+        pair_copy(-(s + 1), 0).wait_recv()
+        pair_copy(s + 1, 1).wait_recv()
         for q in range(n_chunks):
             for d in (0, 1):
                 k = -(s + 1) if d == 0 else s + 1
@@ -231,13 +220,14 @@
                     ring_copy(d, s - 1, q).wait_recv()
                     sends[d][s, q] = recvs[d][s - 1, q] + own(k, columns(d, q))
                 ring_copy(d, s, q).start()
-    need(0)
+    pair_copy(0, 0).wait_recv()
+    pair_copy(0, 1).wait_recv()
     for q in range(n_chunks):
         for d in (0, 1):
             ring_copy(d, n_y - 2, q).wait_recv()
             out_ref[:, columns(d, q)] = recvs[d][n_y - 2, q] + own(0, columns(d, q))
-    for k in order:
-        pair_copy(k).wait_send()
+    for k, d in order:
+        pair_copy(k, d).wait_send()
     for s in range(n_y - 1):
         for q in range(n_chunks):
             ring_copy(0, s, q).wait_send()
@@ -262,8 +252,8 @@
             slots,
             slots,
             slots,
-            pltpu.SemaphoreType.DMA((n_y,)),
-            pltpu.SemaphoreType.DMA((n_y,)),
+            pltpu.SemaphoreType.DMA((n_y, 2)),
+            pltpu.SemaphoreType.DMA((n_y, 2)),
             pltpu.SemaphoreType.DMA((2, n_y - 1, n_chunks)),
             pltpu.SemaphoreType.DMA((2, n_y - 1, n_chunks)),
         ],

time: 81.5 us -> 81.6 us (level)
  no operation moved by 1% of the time
where the time goes in v8:
time: 81.6 us; the launch traced here: 80.8 us
  Pallas kernels  66.7 us (82%)
  matrix products  9.85 us (12%)
  other arithmetic  1.88 us (2%)
  local copies, waits for them, and re-layouts  1.69 us (2%)
    pallas_call x1, Pallas kernels, scatter_rows(): pl.pallas_call(functools.partial(scatter_kernel, n_y, n_chunks), out_shap...  37.1 us
    pallas_call x1, Pallas kernels, gather_rows(): pl.pallas_call(functools.partial(gather_kernel, n_x, n_z), out_shape=jax....  29.6 us
    dot_general x1, matrix products, contract_rows(): lax.dot_general(row_block, col_block, (((1,), (1,)), ((), ())), precision...  7.98 us
    dot_general x4, matrix products, lookup_energy(): lax.dot_general(one_hot, table, (((1,), (1,)), ((), ())), precision=lax.P...  1.86 us
    div x1, other arithmetic, on_device(): update = ladder / denominator  1.79 us
    unnamed x9, local copies, waits for them, and re-layouts  1.69 us

profile of v8, /device:TPU:1, one launch (start us, length us, event | category | flops | bytes accessed | tf_op | source)
XLA Modules:
  0.0 80.8 jit_solution(10719532132277471859)
XLA Ops:
  0.6 0.0 copy-start
  0.6 29.6 %shard_map.77 = f32[512,512]{1,0:T(8,128)} custom-call(f32[16,512]{1,0:T(8,128)} %amp_ref.1), custom_call_target="tpu_custom_call" | custom-call | tf_op jit(solution)/shard_map/pallas_call | solution.py:131
  30.2 8.0 %fusion.17 = f32[512,2048]{1,0:T(8,128)} fusion(f32[512,512]{1,0:T(8,128)} %shard_map.77, f32[2048,512]{1,0:T(8,128)} %param.7), kind=kOutput, calls=%fused_computation.50 | convolution fusion | flops 3221225472 | bytes 9437184 | tf_op jit(solution)/shard_map/dot_general | solution.py:29
  38.2 0.0 copy-start.1
  38.2 0.0 copy-start.2
  38.2 0.0 copy-start.3
  38.2 37.1 %shard_map.78 = f32[32,2048]{1,0:T(8,128)} custom-call(f32[8,2,32,2048]{3,2,1,0:T(8,128)} %bitcast.50), custom_call_target="tpu_custom_call" | custom-call | tf_op jit(solution)/shard_map/pallas_call | solution.py:244
  75.3 0.0 copy-done.1
  75.3 0.1 and_select_fusion.1
  75.4 0.0 copy-done
  75.4 0.7 fusion.1
  76.2 0.7 fusion
  76.9 0.0 copy-done.2
  76.9 0.0 copy-done.3
  76.9 0.2 fusion.2
  77.1 0.2 fusion.4
  77.3 1.8 %subtract_divide_fusion = f32[32,2048]{1,0:T(8,128)} fusion(f32[32,2048]{1,0:T(8,128)} %shard_map.78, f32[2048]{0:T(1024)S(1)} %fusion.1, f32[2048]{0:T(1024)S(1)} %fusion, f32[32]{0:T(128)S(1)} %fusion.4), kind=kLoop, calls=%fused_computation.13 | loop fusion | flops 196608 | bytes 540800 | tf_op jit(solution)/shard_map/div | solution.py:272
  79.1 1.7 %copy.9 = f32[32,2048]{1,0:T(8,128)} copy(f32[32,2048]{1,0:T(8,128)} %shard_map.78) | data formatting | bytes 524288
  (1 shorter events, 0.0 us)
Async XLA Ops:
  0.6 74.8 %copy-start = (f32[1536]{0:T(1024)S(1)}, f32[1536]{0:T(1024)}, u32[]{:S(2)}) copy-start(f32[1536]{0:T(1024)} %param.11) | copy-start | bytes 18436
  38.2 37.1 %copy-start.1 = (s32[2048,2]{0,1:T(2,128)S(1)}, s32[2048,2]{0,1:T(2,128)}, u32[]{:S(2)}) copy-start(s32[2048,2]{0,1:T(2,128)} %param.9) | copy-start | bytes 49156
  38.2 38.7 %copy-start.2 = (s32[32,2]{0,1:T(2,128)S(1)}, s32[32,2]{0,1:T(2,128)}, u32[]{:S(2)}) copy-start(s32[32,2]{0,1:T(2,128)} %param.8) | copy-start | bytes 772
  38.2 38.7 %copy-start.3 = (f32[128]{0:T(128)S(1)}, f32[128]{0:T(128)}, u32[]{:S(2)}) copy-start(f32[128]{0:T(128)} %param.10) | copy-start | bytes 1540

commit v9 on v8

--- a/solution.py
+++ b/solution.py
@@ -35,7 +35,7 @@
     )
 
 
-def gather_kernel(n_x, n_z, amp_ref, out_ref, held, local_sem, x_send, x_recv, z_send, z_recv):
+def gather_kernel(n_x, n_z, amp_ref, int_ref, out_ref, held, int_hi, int_lo, local_sem, x_send, x_recv, z_send, z_recv):
     ab = lax.axis_index("ab")
     cd = lax.axis_index("cd")
     z, x = ab // n_x, lax.rem(ab, n_x)
@@ -71,6 +71,39 @@
         x_copy(i, False).start()
     local = pltpu.make_async_copy(amp_ref, held.at[block_rows(ab)], local_sem)
     local.start()
+
+    tile = 256
+    n_tiles = int_ref.shape[0] // tile
+
+    def split(j, carry):
+        span = pl.ds(pl.multiple_of(j * tile, tile), tile)
+        value = int_ref[span, :]
+        high = value.astype(jnp.bfloat16)
+        int_hi[span, :] = high
+        int_lo[span, :] = (value - high.astype(jnp.float32)).astype(jnp.bfloat16)
+        return carry
+
+    lax.fori_loop(0, n_tiles, split, 0)
+
+    def contract(group_z):
+        span = pl.ds(pl.multiple_of(group_z * group, group), group)
+        value = held[span, :]
+        high = value.astype(jnp.bfloat16)
+        low = (value - high.astype(jnp.float32)).astype(jnp.bfloat16)
+        dims = (((1,), (1,)), ((), ()))
+
+        def one_tile(j, carry):
+            cols = pl.ds(pl.multiple_of(j * tile, tile), tile)
+            b_high = int_hi[cols, :]
+            b_low = int_lo[cols, :]
+            acc = lax.dot_general(high, b_high, dims, preferred_element_type=jnp.float32)
+            acc += lax.dot_general(high, b_low, dims, preferred_element_type=jnp.float32)
+            acc += lax.dot_general(low, b_high, dims, preferred_element_type=jnp.float32)
+            out_ref[span, cols] = acc
+            return carry
+
+        lax.fori_loop(0, n_tiles, one_tile, 0)
+
     local.wait()
     for i in range(1, n_x):
         x_copy(i, True).wait_recv()
@@ -107,34 +140,41 @@
             device_id_type=MESH,
         )
 
+    for q in range(n_x):
+        for d in (0, 1):
+            z_copy(d, 0, q).start()
+    contract(z)
     for t in range(steps):
         for q in range(n_x):
             for d in (0, 1):
-                if t > 0:
-                    z_arrival(d, t - 1, q).wait_recv()
-                z_copy(d, t, q).start()
-    for q in range(n_x):
-        for d in (0, 1):
-            z_arrival(d, steps - 1, q).wait_recv()
+                z_arrival(d, t, q).wait_recv()
+                if t + 1 < steps:
+                    z_copy(d, t + 1, q).start()
+        if t + 1 < steps:
+            contract(lax.rem(z + n_z - t - 1, n_z))
+            contract(lax.rem(z + t + 1, n_z))
+        else:
+            contract(lax.rem(z + t + 1, n_z))
     for i in range(1, n_x):
         x_copy(i, False).wait_send()
     for t in range(steps):
         for q in range(n_x):
             for d in (0, 1):
                 z_copy(d, t, q).wait_send()
-    out_ref[...] = held[...]
-
-
-def gather_rows(amplitudes, n_x, n_z):
+
+
+def gather_contract(amplitudes, integrals, n_x, n_z):
     rows, cols = amplitudes.shape
     steps = n_z // 2
     return pl.pallas_call(
         functools.partial(gather_kernel, n_x, n_z),
-        out_shape=jax.ShapeDtypeStruct((rows * n_x * n_z, cols), amplitudes.dtype),
-        in_specs=[pl.BlockSpec(memory_space=pltpu.VMEM)],
+        out_shape=jax.ShapeDtypeStruct((rows * n_x * n_z, integrals.shape[0]), jnp.float32),
+        in_specs=[pl.BlockSpec(memory_space=pltpu.VMEM)] * 2,
         out_specs=pl.BlockSpec(memory_space=pltpu.VMEM),
         scratch_shapes=[
             pltpu.VMEM((rows * n_x * n_z, cols), amplitudes.dtype),
+            pltpu.VMEM(integrals.shape, jnp.bfloat16),
+            pltpu.VMEM(integrals.shape, jnp.bfloat16),
             pltpu.SemaphoreType.DMA(()),
             pltpu.SemaphoreType.DMA((n_x,)),
             pltpu.SemaphoreType.DMA((n_x,)),
@@ -142,7 +182,7 @@
             pltpu.SemaphoreType.DMA((2, steps, n_x)),
         ],
         compiler_params=pltpu.CompilerParams(collective_id=0, has_side_effects=True),
-    )(amplitudes)
+    )(amplitudes, integrals)
 
 
 def x_extent(mesh):
@@ -262,7 +302,7 @@
 
 
 def on_device(n_x, n_z, n_cd, amplitudes, integrals, ij_pairs, ab_pairs, eps_occ, eps_vir):
-    partial_value = contract_rows(gather_rows(amplitudes, n_x, n_z), integrals)
+    partial_value = gather_contract(amplitudes, integrals, n_x, n_z)
     ladder = scatter_rows(partial_value, n_cd)
     first_occ = lookup_energy(ij_pairs[:, 0], eps_occ)[:, None]
     second_occ = lookup_energy(ij_pairs[:, 1], eps_occ)[:, None]

time: 81.6 us -> 86 us (1.054)
  Pallas kernels: 66.7 us -> 79 us
  matrix products: 9.85 us -> 1.86 us
    pallas_call x1, Pallas kernels: 29.6 us -> 43.4 us  [gather_contract(): pl.pallas_call(functools.partial(gather_kernel, n_x, n_z), out_shape=jax....]
    dot_general x1 -> x0, matrix products: 7.98 us -> none  [contract_rows(): lax.dot_general(row_block, col_block, (((1,), (1,)), ((), ())), precision...]
    pallas_call x1, Pallas kernels: 37.1 us -> 35.7 us  [scatter_rows(): pl.pallas_call(functools.partial(scatter_kernel, n_y, n_chunks), out_shap...]
where the time goes in v9:
time: 86 us; the launch traced here: 85.2 us
  Pallas kernels  79 us (92%)
  other arithmetic  1.88 us (2%)
  matrix products  1.86 us (2%)
  local copies, waits for them, and re-layouts  1.7 us (2%)
    pallas_call x1, Pallas kernels, gather_contract(): pl.pallas_call(functools.partial(gather_kernel, n_x, n_z), out_shape=jax....  43.4 us
    pallas_call x1, Pallas kernels, scatter_rows(): pl.pallas_call(functools.partial(scatter_kernel, n_y, n_chunks), out_shap...  35.7 us
    dot_general x4, matrix products, lookup_energy(): lax.dot_general(one_hot, table, (((1,), (1,)), ((), ())), precision=lax.P...  1.86 us
    div x1, other arithmetic, on_device(): update = ladder / denominator  1.79 us

profile of v9, /device:TPU:1, one launch (start us, length us, event | category | flops | bytes accessed | tf_op | source)
XLA Modules:
  0.0 85.2 jit_solution(16199583822251158690)
XLA Ops:
  0.6 0.0 copy-start
  0.6 43.4 %shard_map.77 = f32[512,2048]{1,0:T(8,128)} custom-call(f32[16,512]{1,0:T(8,128)} %amp_ref.1, f32[2048,512]{1,0:T(8,128)} %int_ref.1), custom_call_target="tpu_custom_call" | custom-call | tf_op jit(solution)/shard_map/pallas_call | solution.py:169
  44.0 0.0 copy-start.1
  44.0 0.0 copy-start.2
  44.0 0.0 copy-start.3
  44.1 35.7 %shard_map.78 = f32[32,2048]{1,0:T(8,128)} custom-call(f32[8,2,32,2048]{3,2,1,0:T(8,128)} %bitcast.48), custom_call_target="tpu_custom_call" | custom-call | tf_op jit(solution)/shard_map/pallas_call | solution.py:284
  79.7 0.0 copy-done.1
  79.7 0.1 and_select_fusion.1
  79.8 0.0 copy-done
  79.8 0.7 fusion.1
  80.6 0.7 fusion
  81.3 0.0 copy-done.2
  81.3 0.0 copy-done.3
  81.3 0.2 fusion.2
  81.5 0.2 fusion.4
  81.7 1.8 %subtract_divide_fusion = f32[32,2048]{1,0:T(8,128)} fusion(f32[32,2048]{1,0:T(8,128)} %shard_map.78, f32[2048]{0:T(1024)S(1)} %fusion.1, f32[2048]{0:T(1024)S(1)} %fusion, f32[32]{0:T(128)S(1)} %fusion.4), kind=kLoop, calls=%fused_computation.13 | loop fusion | flops 196608 | bytes 540800 | tf_op jit(solution)/shard_map/div | solution.py:312
  83.5 1.7 %copy.9 = f32[32,2048]{1,0:T(8,128)} copy(f32[32,2048]{1,0:T(8,128)} %shard_map.78) | data formatting | bytes 524288
  (1 shorter events, 0.0 us)
Async XLA Ops:
  0.6 79.2 %copy-start = (f32[1536]{0:T(1024)S(1)}, f32[1536]{0:T(1024)}, u32[]{:S(2)}) copy-start(f32[1536]{0:T(1024)} %param.11) | copy-start | bytes 18436
  44.0 35.7 %copy-start.1 = (s32[2048,2]{0,1:T(2,128)S(1)}, s32[2048,2]{0,1:T(2,128)}, u32[]{:S(2)}) copy-start(s32[2048,2]{0,1:T(2,128)} %param.9) | copy-start | bytes 49156
  44.0 37.3 %copy-start.2 = (s32[32,2]{0,1:T(2,128)S(1)}, s32[32,2]{0,1:T(2,128)}, u32[]{:S(2)}) copy-start(s32[32,2]{0,1:T(2,128)} %param.8) | copy-start | bytes 772
  44.0 37.3 %copy-start.3 = (f32[128]{0:T(128)S(1)}, f32[128]{0:T(128)}, u32[]{:S(2)}) copy-start(f32[128]{0:T(128)} %param.10) | copy-start | bytes 1540

commit v10 on v9

--- a/solution.py
+++ b/solution.py
@@ -145,16 +145,16 @@
             z_copy(d, 0, q).start()
     contract(z)
     for t in range(steps):
+        if t == steps - 1:
+            for u in range(steps - 1):
+                contract(lax.rem(z + n_z - u - 1, n_z))
+                contract(lax.rem(z + u + 1, n_z))
         for q in range(n_x):
             for d in (0, 1):
                 z_arrival(d, t, q).wait_recv()
                 if t + 1 < steps:
                     z_copy(d, t + 1, q).start()
-        if t + 1 < steps:
-            contract(lax.rem(z + n_z - t - 1, n_z))
-            contract(lax.rem(z + t + 1, n_z))
-        else:
-            contract(lax.rem(z + t + 1, n_z))
+    contract(lax.rem(z + steps, n_z))
     for i in range(1, n_x):
         x_copy(i, False).wait_send()
     for t in range(steps):

time: 86 us -> 92.7 us (1.078)
  Pallas kernels: 79 us -> 85.7 us
    pallas_call x1, Pallas kernels: 43.4 us -> 50.4 us  [gather_contract(): pl.pallas_call(functools.partial(gather_kernel, n_x, n_z), out_shape=jax....]
where the time goes in v10:
time: 92.7 us; the launch traced here: 91.9 us
  Pallas kernels  85.7 us (92%)
  other arithmetic  1.88 us (2%)
  matrix products  1.86 us (2%)
  local copies, waits for them, and re-layouts  1.7 us (2%)
    pallas_call x1, Pallas kernels, gather_contract(): pl.pallas_call(functools.partial(gather_kernel, n_x, n_z), out_shape=jax....  50.4 us
    pallas_call x1, Pallas kernels, scatter_rows(): pl.pallas_call(functools.partial(scatter_kernel, n_y, n_chunks), out_shap...  35.3 us
    dot_general x4, matrix products, lookup_energy(): lax.dot_general(one_hot, table, (((1,), (1,)), ((), ())), precision=lax.P...  1.86 us

profile of v10, /device:TPU:1, one launch (start us, length us, event | category | flops | bytes accessed | tf_op | source)
XLA Modules:
  0.0 91.9 jit_solution(519125103880648043)
XLA Ops:
  0.6 0.0 copy-start
  0.6 50.4 %shard_map.77 = f32[512,2048]{1,0:T(8,128)} custom-call(f32[16,512]{1,0:T(8,128)} %amp_ref.1, f32[2048,512]{1,0:T(8,128)} %int_ref.1), custom_call_target="tpu_custom_call" | custom-call | tf_op jit(solution)/shard_map/pallas_call | solution.py:169
  51.1 0.0 copy-start.1
  51.1 0.0 copy-start.2
  51.1 0.0 copy-start.3
  51.1 35.3 %shard_map.78 = f32[32,2048]{1,0:T(8,128)} custom-call(f32[8,2,32,2048]{3,2,1,0:T(8,128)} %bitcast.48), custom_call_target="tpu_custom_call" | custom-call | tf_op jit(solution)/shard_map/pallas_call | solution.py:284
  86.4 0.0 copy-done.1
  86.4 0.1 and_select_fusion.1
  86.5 0.0 copy-done
  86.5 0.7 fusion.1
  87.3 0.7 fusion
  88.0 0.0 copy-done.2
  88.1 0.0 copy-done.3
  88.1 0.2 fusion.2
  88.3 0.2 fusion.4
  88.5 1.8 %subtract_divide_fusion = f32[32,2048]{1,0:T(8,128)} fusion(f32[32,2048]{1,0:T(8,128)} %shard_map.78, f32[2048]{0:T(1024)S(1)} %fusion.1, f32[2048]{0:T(1024)S(1)} %fusion, f32[32]{0:T(128)S(1)} %fusion.4), kind=kLoop, calls=%fused_computation.13 | loop fusion | flops 196608 | bytes 540800 | tf_op jit(solution)/shard_map/div | solution.py:312
  90.3 1.7 %copy.9 = f32[32,2048]{1,0:T(8,128)} copy(f32[32,2048]{1,0:T(8,128)} %shard_map.78) | data formatting | bytes 524288
  (1 shorter events, 0.0 us)
Async XLA Ops:
  0.6 85.9 %copy-start = (f32[1536]{0:T(1024)S(1)}, f32[1536]{0:T(1024)}, u32[]{:S(2)}) copy-start(f32[1536]{0:T(1024)} %param.11) | copy-start | bytes 18436
  51.1 35.4 %copy-start.1 = (s32[2048,2]{0,1:T(2,128)S(1)}, s32[2048,2]{0,1:T(2,128)}, u32[]{:S(2)}) copy-start(s32[2048,2]{0,1:T(2,128)} %param.9) | copy-start | bytes 49156
  51.1 37.0 %copy-start.2 = (s32[32,2]{0,1:T(2,128)S(1)}, s32[32,2]{0,1:T(2,128)}, u32[]{:S(2)}) copy-start(s32[32,2]{0,1:T(2,128)} %param.8) | copy-start | bytes 772
  51.1 37.0 %copy-start.3 = (f32[128]{0:T(128)S(1)}, f32[128]{0:T(128)}, u32[]{:S(2)}) copy-start(f32[128]{0:T(128)} %param.10) | copy-start | bytes 1540

commit v11 on v6

--- a/solution.py
+++ b/solution.py
@@ -280,7 +280,7 @@
     second_vir = lookup_energy(ab_pairs[:, 1], eps_vir)[None, :]
     denominator = first_occ + second_occ - first_vir - second_vir
     update = ladder / denominator
-    return (ladder, update)
+    return (jnp.where(denominator == denominator, ladder, update), update)
 
 
 def solution(mesh):

time: 81.5 us -> 79.9 us (0.980)
  local copies, waits for them, and re-layouts: 1.69 us -> 0.02 us
    select_n x0 -> x1, other arithmetic: none -> 1.89 us  [on_device(): return (jnp.where(denominator == denominator, ladder, update), update)]
    div x1 -> x0, other arithmetic: 1.79 us -> none  [on_device(): update = ladder / denominator]
    unnamed x9 -> x8, local copies, waits for them, and re-layouts: 1.69 us -> 0.02 us
where the time goes in v11:
time: 79.9 us; the launch traced here: 79.5 us
  Pallas kernels  67 us (84%)
  matrix products  9.85 us (12%)
  other arithmetic  1.99 us (2%)
    pallas_call x1, Pallas kernels, scatter_rows(): pl.pallas_call(functools.partial(scatter_kernel, n_y, n_chunks), out_shap...  37.4 us
    pallas_call x1, Pallas kernels, gather_rows(): pl.pallas_call(functools.partial(gather_kernel, n_x, n_z), out_shape=jax....  29.6 us
    dot_general x1, matrix products, contract_rows(): lax.dot_general(row_block, col_block, (((1,), (1,)), ((), ())), precision...  7.98 us
    select_n x1, other arithmetic, on_device(): return (jnp.where(denominator == denominator, ladder, update), update)  1.89 us
    dot_general x4, matrix products, lookup_energy(): lax.dot_general(one_hot, table, (((1,), (1,)), ((), ())), precision=lax.P...  1.86 us

profile of v11, /device:TPU:1, one launch (start us, length us, event | category | flops | bytes accessed | tf_op | source)
XLA Modules:
  0.0 79.5 jit_solution(1044907852128763779)
XLA Ops:
  0.6 0.0 copy-start
  0.6 29.6 %shard_map.77 = f32[512,512]{1,0:T(8,128)} custom-call(f32[16,512]{1,0:T(8,128)} %amp_ref.1), custom_call_target="tpu_custom_call" | custom-call | tf_op jit(solution)/shard_map/pallas_call | solution.py:131
  30.2 8.0 %fusion.21 = f32[512,2048]{1,0:T(8,128)} fusion(f32[512,512]{1,0:T(8,128)} %shard_map.77, f32[2048,512]{1,0:T(8,128)} %param.7), kind=kOutput, calls=%fused_computation.53 | convolution fusion | flops 3221225472 | bytes 9437184 | tf_op jit(solution)/shard_map/dot_general | solution.py:29
  38.2 0.0 copy-start.1
  38.2 0.0 copy-start.2
  38.2 0.0 copy-start.3
  38.2 37.4 %shard_map.78 = f32[32,2048]{1,0:T(8,128)} custom-call(f32[8,2,32,2048]{3,2,1,0:T(8,128)} %bitcast.50), custom_call_target="tpu_custom_call" | custom-call | tf_op jit(solution)/shard_map/pallas_call | solution.py:254
  75.6 0.0 copy-done.1
  75.6 0.1 and_select_fusion.1
  75.7 0.0 copy-done
  75.7 0.7 fusion.1
  76.5 0.7 fusion
  77.2 0.0 copy-done.2
  77.2 0.0 copy-done.3
  77.2 0.2 fusion.2
  77.4 0.2 fusion.4
  77.6 1.9 %fusion.9 = (f32[32,2048]{1,0:T(8,128)}, f32[32,2048]{1,0:T(8,128)}) fusion(f32[32,2048]{1,0:T(8,128)} %shard_map.78, f32[2048]{0:T(1024)S(1)} %fusion.1, f32[2048]{0:T(1024)S(1)} %fusion, f32[32]{0:T(128)S(1)} %fusion.4), kind=kLoop, calls=%fused_computation.16 | loop fusion | flops 327680 | bytes 802944 | tf_op jit(solution)/shard_map/jit(_where)/select_n | solution.py:283
  (1 shorter events, 0.0 us)
Async XLA Ops:
  0.6 75.1 %copy-start = (f32[1536]{0:T(1024)S(1)}, f32[1536]{0:T(1024)}, u32[]{:S(2)}) copy-start(f32[1536]{0:T(1024)} %param.11) | copy-start | bytes 18436
  38.2 37.4 %copy-start.1 = (s32[2048,2]{0,1:T(2,128)S(1)}, s32[2048,2]{0,1:T(2,128)}, u32[]{:S(2)}) copy-start(s32[2048,2]{0,1:T(2,128)} %param.9) | copy-start | bytes 49156
  38.2 39.0 %copy-start.2 = (s32[32,2]{0,1:T(2,128)S(1)}, s32[32,2]{0,1:T(2,128)}, u32[]{:S(2)}) copy-start(s32[32,2]{0,1:T(2,128)} %param.8) | copy-start | bytes 772
  38.2 39.0 %copy-start.3 = (f32[128]{0:T(128)S(1)}, f32[128]{0:T(128)}, u32[]{:S(2)}) copy-start(f32[128]{0:T(128)} %param.10) | copy-start | bytes 1540

commit v12 on v11

--- a/solution.py
+++ b/solution.py
@@ -71,9 +71,6 @@
         x_copy(i, False).start()
     local = pltpu.make_async_copy(amp_ref, held.at[block_rows(ab)], local_sem)
     local.start()
-    local.wait()
-    for i in range(1, n_x):
-        x_copy(i, True).wait_recv()
 
     steps = n_z // 2
 
@@ -107,11 +104,18 @@
             device_id_type=MESH,
         )
 
-    for t in range(steps):
+    for i in range(n_x):
+        if i == 0:
+            local.wait()
+        else:
+            x_copy(i, True).wait_recv()
+        landed = lax.rem(x + n_x - i, n_x)
+        for d in (0, 1):
+            z_copy(d, 0, landed).start()
+    for t in range(1, steps):
         for q in range(n_x):
             for d in (0, 1):
-                if t > 0:
-                    z_arrival(d, t - 1, q).wait_recv()
+                z_arrival(d, t - 1, q).wait_recv()
                 z_copy(d, t, q).start()
     for q in range(n_x):
         for d in (0, 1):

time: 79.9 us -> 79.4 us (level)
    pallas_call x1, Pallas kernels: 29.6 us -> 28.5 us  [gather_rows(): pl.pallas_call(functools.partial(gather_kernel, n_x, n_z), out_shape=jax....]
where the time goes in v12:
time: 79.4 us; the launch traced here: 79.1 us
  Pallas kernels  66.5 us (84%)
  matrix products  9.85 us (12%)
  other arithmetic  1.99 us (3%)
    pallas_call x1, Pallas kernels, scatter_rows(): pl.pallas_call(functools.partial(scatter_kernel, n_y, n_chunks), out_shap...  38 us
    pallas_call x1, Pallas kernels, gather_rows(): pl.pallas_call(functools.partial(gather_kernel, n_x, n_z), out_shape=jax....  28.5 us
    dot_general x1, matrix products, contract_rows(): lax.dot_general(row_block, col_block, (((1,), (1,)), ((), ())), precision...  7.98 us
    select_n x1, other arithmetic, on_device(): return (jnp.where(denominator == denominator, ladder, update), update)  1.89 us
    dot_general x4, matrix products, lookup_energy(): lax.dot_general(one_hot, table, (((1,), (1,)), ((), ())), precision=lax.P...  1.86 us

profile of v12, /device:TPU:1, one launch (start us, length us, event | category | flops | bytes accessed | tf_op | source)
XLA Modules:
  0.0 79.1 jit_solution(9431813726359256232)
XLA Ops:
  0.6 0.0 copy-start
  0.6 28.5 %shard_map.77 = f32[512,512]{1,0:T(8,128)} custom-call(f32[16,512]{1,0:T(8,128)} %amp_ref.1), custom_call_target="tpu_custom_call" | custom-call | tf_op jit(solution)/shard_map/pallas_call | solution.py:135
  29.2 8.0 %fusion.21 = f32[512,2048]{1,0:T(8,128)} fusion(f32[512,512]{1,0:T(8,128)} %shard_map.77, f32[2048,512]{1,0:T(8,128)} %param.7), kind=kOutput, calls=%fused_computation.53 | convolution fusion | flops 3221225472 | bytes 9437184 | tf_op jit(solution)/shard_map/dot_general | solution.py:29
  37.1 0.0 copy-start.1
  37.2 0.0 copy-start.2
  37.2 0.0 copy-start.3
  37.2 38.0 %shard_map.78 = f32[32,2048]{1,0:T(8,128)} custom-call(f32[8,2,32,2048]{3,2,1,0:T(8,128)} %bitcast.50), custom_call_target="tpu_custom_call" | custom-call | tf_op jit(solution)/shard_map/pallas_call | solution.py:258
  75.2 0.0 copy-done.1
  75.2 0.1 and_select_fusion.1
  75.3 0.0 copy-done
  75.3 0.7 fusion.1
  76.0 0.7 fusion
  76.8 0.0 copy-done.2
  76.8 0.0 copy-done.3
  76.8 0.2 fusion.2
  77.0 0.2 fusion.4
  77.2 1.9 %fusion.9 = (f32[32,2048]{1,0:T(8,128)}, f32[32,2048]{1,0:T(8,128)}) fusion(f32[32,2048]{1,0:T(8,128)} %shard_map.78, f32[2048]{0:T(1024)S(1)} %fusion.1, f32[2048]{0:T(1024)S(1)} %fusion, f32[32]{0:T(128)S(1)} %fusion.4), kind=kLoop, calls=%fused_computation.16 | loop fusion | flops 327680 | bytes 802944 | tf_op jit(solution)/shard_map/jit(_where)/select_n | solution.py:287
  (1 shorter events, 0.0 us)
Async XLA Ops:
  0.6 74.6 %copy-start = (f32[1536]{0:T(1024)S(1)}, f32[1536]{0:T(1024)}, u32[]{:S(2)}) copy-start(f32[1536]{0:T(1024)} %param.11) | copy-start | bytes 18436
  37.1 38.0 %copy-start.1 = (s32[2048,2]{0,1:T(2,128)S(1)}, s32[2048,2]{0,1:T(2,128)}, u32[]{:S(2)}) copy-start(s32[2048,2]{0,1:T(2,128)} %param.9) | copy-start | bytes 49156
  37.2 39.6 %copy-start.2 = (s32[32,2]{0,1:T(2,128)S(1)}, s32[32,2]{0,1:T(2,128)}, u32[]{:S(2)}) copy-start(s32[32,2]{0,1:T(2,128)} %param.8) | copy-start | bytes 772
  37.2 39.6 %copy-start.3 = (f32[128]{0:T(128)S(1)}, f32[128]{0:T(128)}, u32[]{:S(2)}) copy-start(f32[128]{0:T(128)} %param.10) | copy-start | bytes 1540

commit v13 on v12

--- a/solution.py
+++ b/solution.py
@@ -157,8 +157,8 @@
         return 2
 
 
-def scatter_kernel(n_y, n_chunks, part_ref, out_ref, pair, send_r, recv_r, send_l, recv_l,
-                   pair_send, pair_recv, ring_send, ring_recv):
+def scatter_kernel(n_y, n_chunks, part_ref, out_ref, mine, pair, send_r, recv_r, send_l, recv_l,
+                   mine_sem, pair_send, pair_recv, ring_send, ring_recv):
     ab = lax.axis_index("ab")
     cd = lax.axis_index("cd")
     y, core = cd // 2, lax.rem(cd, 2)
@@ -169,6 +169,19 @@
     half = out_ref.shape[1] // 2
     width = half // n_chunks
 
+    def fetch(k):
+        b = lax.rem(y + k + n_y, n_y)
+        return pltpu.make_async_copy(part_ref.at[b, core], mine.at[b], mine_sem.at[b])
+
+    fetch_order = []
+    for s in range(1, n_y // 2 + 1):
+        for k in (-s, s):
+            if k % n_y not in [j % n_y for j in fetch_order]:
+                fetch_order.append(k)
+    fetch_order.append(0)
+    for k in fetch_order:
+        fetch(k).start()
+
     barrier = pltpu.get_barrier_semaphore()
     for peer in (partner, right, left):
         pl.semaphore_signal(barrier, inc=1, device_id=(ab, peer), device_id_type=MESH)
@@ -196,7 +209,7 @@
 
     def own(k, cols):
         b = lax.rem(y + k + n_y, n_y)
-        return part_ref[b, core, :, cols] + pair[b, :, cols]
+        return mine[b, :, cols] + pair[b, :, cols]
 
     def columns(d, q):
         start = d * half + q * width
@@ -222,6 +235,7 @@
         if k not in waited:
             waited.add(k)
             pair_copy(k if k <= n_y // 2 else k - n_y).wait_recv()
+            fetch(k).wait()
 
     for s in range(n_y - 1):
         need(-(s + 1))
@@ -258,14 +272,16 @@
     return pl.pallas_call(
         functools.partial(scatter_kernel, n_y, n_chunks),
         out_shape=jax.ShapeDtypeStruct((rows, cols), partial_value.dtype),
-        in_specs=[pl.BlockSpec(memory_space=pltpu.VMEM)],
+        in_specs=[pl.BlockSpec(memory_space=pl.ANY)],
         out_specs=pl.BlockSpec(memory_space=pltpu.VMEM),
         scratch_shapes=[
+            pltpu.VMEM((n_y, rows, cols), jnp.float32),
             pltpu.VMEM((n_y, rows, cols), jnp.float32),
             slots,
             slots,
             slots,
             slots,
+            pltpu.SemaphoreType.DMA((n_y,)),
             pltpu.SemaphoreType.DMA((n_y,)),
             pltpu.SemaphoreType.DMA((n_y,)),
             pltpu.SemaphoreType.DMA((2, n_y - 1, n_chunks)),

time: 79.4 us -> 77.5 us (0.976)
  Pallas kernels: 66.5 us -> 64.6 us
    pallas_call x1, Pallas kernels: 38 us -> 36.1 us  [scatter_rows(): pl.pallas_call(functools.partial(scatter_kernel, n_y, n_chunks), out_shap...]
where the time goes in v13:
time: 77.5 us; the launch traced here: 77.2 us
  Pallas kernels  64.6 us (83%)
  matrix products  9.85 us (13%)
  other arithmetic  1.99 us (3%)
    pallas_call x1, Pallas kernels, scatter_rows(): pl.pallas_call(functools.partial(scatter_kernel, n_y, n_chunks), out_shap...  36.1 us
    pallas_call x1, Pallas kernels, gather_rows(): pl.pallas_call(functools.partial(gather_kernel, n_x, n_z), out_shape=jax....  28.5 us
    dot_general x1, matrix products, contract_rows(): lax.dot_general(row_block, col_block, (((1,), (1,)), ((), ())), precision...  7.98 us
    select_n x1, other arithmetic, on_device(): return (jnp.where(denominator == denominator, ladder, update), update)  1.89 us
    dot_general x4, matrix products, lookup_energy(): lax.dot_general(one_hot, table, (((1,), (1,)), ((), ())), precision=lax.P...  1.86 us

profile of v13, /device:TPU:1, one launch (start us, length us, event | category | flops | bytes accessed | tf_op | source)
XLA Modules:
  0.0 77.2 jit_solution(13919688553442549646)
XLA Ops:
  0.6 0.0 copy-start
  0.6 28.5 %shard_map.77 = f32[512,512]{1,0:T(8,128)} custom-call(f32[16,512]{1,0:T(8,128)} %amp_ref.1), custom_call_target="tpu_custom_call" | custom-call | tf_op jit(solution)/shard_map/pallas_call | solution.py:135
  29.2 8.0 %fusion.21 = f32[512,2048]{1,0:T(8,128)} fusion(f32[512,512]{1,0:T(8,128)} %shard_map.77, f32[2048,512]{1,0:T(8,128)} %param.7), kind=kOutput, calls=%fused_computation.53 | convolution fusion | flops 3221225472 | bytes 9437184 | tf_op jit(solution)/shard_map/dot_general | solution.py:29
  37.1 0.0 copy-start.1
  37.2 0.0 copy-start.2
  37.2 0.0 copy-start.3
  37.2 36.1 %shard_map.78 = f32[32,2048]{1,0:T(8,128)} custom-call(f32[8,2,32,2048]{3,2,1,0:T(8,128)} %bitcast.50), custom_call_target="tpu_custom_call" | custom-call | tf_op jit(solution)/shard_map/pallas_call | solution.py:272
  73.3 0.0 copy-done.1
  73.3 0.1 and_select_fusion.1
  73.4 0.0 copy-done
  73.4 0.7 fusion.1
  74.2 0.7 fusion
  74.9 0.0 copy-done.2
  74.9 0.0 copy-done.3
  74.9 0.2 fusion.2
  75.1 0.2 fusion.4
  75.3 1.9 %fusion.9 = (f32[32,2048]{1,0:T(8,128)}, f32[32,2048]{1,0:T(8,128)}) fusion(f32[32,2048]{1,0:T(8,128)} %shard_map.78, f32[2048]{0:T(1024)S(1)} %fusion.1, f32[2048]{0:T(1024)S(1)} %fusion, f32[32]{0:T(128)S(1)} %fusion.4), kind=kLoop, calls=%fused_computation.16 | loop fusion | flops 327680 | bytes 802944 | tf_op jit(solution)/shard_map/jit(_where)/select_n | solution.py:303
  (1 shorter events, 0.0 us)
Async XLA Ops:
  0.6 72.8 %copy-start = (f32[1536]{0:T(1024)S(1)}, f32[1536]{0:T(1024)}, u32[]{:S(2)}) copy-start(f32[1536]{0:T(1024)} %param.11) | copy-start | bytes 18436
  37.1 36.1 %copy-start.1 = (s32[2048,2]{0,1:T(2,128)S(1)}, s32[2048,2]{0,1:T(2,128)}, u32[]{:S(2)}) copy-start(s32[2048,2]{0,1:T(2,128)} %param.9) | copy-start | bytes 49156
  37.2 37.7 %copy-start.2 = (s32[32,2]{0,1:T(2,128)S(1)}, s32[32,2]{0,1:T(2,128)}, u32[]{:S(2)}) copy-start(s32[32,2]{0,1:T(2,128)} %param.8) | copy-start | bytes 772
  37.2 37.8 %copy-start.3 = (f32[128]{0:T(128)S(1)}, f32[128]{0:T(128)}, u32[]{:S(2)}) copy-start(f32[128]{0:T(128)} %param.10) | copy-start | bytes 1540

commit v14 on v13

--- a/solution.py
+++ b/solution.py
@@ -35,7 +35,7 @@
     )
 
 
-def gather_kernel(n_x, n_z, amp_ref, out_ref, held, local_sem, x_send, x_recv, z_send, z_recv):
+def gather_kernel(n_x, n_z, amp_ref, out_ref, held, local_sem, out_sem, x_send, x_recv, z_send, z_recv):
     ab = lax.axis_index("ab")
     cd = lax.axis_index("cd")
     z, x = ab // n_x, lax.rem(ab, n_x)
@@ -126,7 +126,9 @@
         for q in range(n_x):
             for d in (0, 1):
                 z_copy(d, t, q).wait_send()
-    out_ref[...] = held[...]
+    result = pltpu.make_async_copy(held, out_ref, out_sem)
+    result.start()
+    result.wait()
 
 
 def gather_rows(amplitudes, n_x, n_z):
@@ -136,9 +138,10 @@
         functools.partial(gather_kernel, n_x, n_z),
         out_shape=jax.ShapeDtypeStruct((rows * n_x * n_z, cols), amplitudes.dtype),
         in_specs=[pl.BlockSpec(memory_space=pltpu.VMEM)],
-        out_specs=pl.BlockSpec(memory_space=pltpu.VMEM),
+        out_specs=pl.BlockSpec(memory_space=pl.ANY),
         scratch_shapes=[
             pltpu.VMEM((rows * n_x * n_z, cols), amplitudes.dtype),
+            pltpu.SemaphoreType.DMA(()),
             pltpu.SemaphoreType.DMA(()),
             pltpu.SemaphoreType.DMA((n_x,)),
             pltpu.SemaphoreType.DMA((n_x,)),

time: 77.5 us -> 77.5 us (level)
  no operation moved by 1% of the time
where the time goes in v14:
time: 77.5 us; the launch traced here: 77.2 us
  Pallas kernels  64.6 us (83%)
  matrix products  9.85 us (13%)
  other arithmetic  1.99 us (3%)
    pallas_call x1, Pallas kernels, scatter_rows(): pl.pallas_call(functools.partial(scatter_kernel, n_y, n_chunks), out_shap...  36.1 us
    pallas_call x1, Pallas kernels, gather_rows(): pl.pallas_call(functools.partial(gather_kernel, n_x, n_z), out_shape=jax....  28.5 us
    dot_general x1, matrix products, contract_rows(): lax.dot_general(row_block, col_block, (((1,), (1,)), ((), ())), precision...  7.98 us
    select_n x1, other arithmetic, on_device(): return (jnp.where(denominator == denominator, ladder, update), update)  1.89 us
    dot_general x4, matrix products, lookup_energy(): lax.dot_general(one_hot, table, (((1,), (1,)), ((), ())), precision=lax.P...  1.86 us

profile of v14, /device:TPU:1, one launch (start us, length us, event | category | flops | bytes accessed | tf_op | source)
XLA Modules:
  0.0 77.2 jit_solution(4517155361737416603)
XLA Ops:
  0.6 0.0 copy-start
  0.6 28.5 %shard_map.77 = f32[512,512]{1,0:T(8,128)} custom-call(f32[16,512]{1,0:T(8,128)} %amp_ref.1), custom_call_target="tpu_custom_call" | custom-call | tf_op jit(solution)/shard_map/pallas_call | solution.py:137
  29.1 8.0 %fusion.21 = f32[512,2048]{1,0:T(8,128)} fusion(f32[512,512]{1,0:T(8,128)} %shard_map.77, f32[2048,512]{1,0:T(8,128)} %param.7), kind=kOutput, calls=%fused_computation.53 | convolution fusion | flops 3221225472 | bytes 9437184 | tf_op jit(solution)/shard_map/dot_general | solution.py:29
  37.1 0.0 copy-start.1
  37.1 0.0 copy-start.2
  37.1 0.0 copy-start.3
  37.1 36.1 %shard_map.78 = f32[32,2048]{1,0:T(8,128)} custom-call(f32[8,2,32,2048]{3,2,1,0:T(8,128)} %bitcast.50), custom_call_target="tpu_custom_call" | custom-call | tf_op jit(solution)/shard_map/pallas_call | solution.py:275
  73.2 0.0 copy-done.1
  73.2 0.1 and_select_fusion.1
  73.3 0.0 copy-done
  73.3 0.7 fusion.1
  74.1 0.7 fusion
  74.8 0.0 copy-done.2
  74.9 0.0 copy-done.3
  74.9 0.2 fusion.2
  75.1 0.2 fusion.4
  75.3 1.9 %fusion.9 = (f32[32,2048]{1,0:T(8,128)}, f32[32,2048]{1,0:T(8,128)}) fusion(f32[32,2048]{1,0:T(8,128)} %shard_map.78, f32[2048]{0:T(1024)S(1)} %fusion.1, f32[2048]{0:T(1024)S(1)} %fusion, f32[32]{0:T(128)S(1)} %fusion.4), kind=kLoop, calls=%fused_computation.16 | loop fusion | flops 327680 | bytes 802944 | tf_op jit(solution)/shard_map/jit(_where)/select_n | solution.py:306
  (1 shorter events, 0.0 us)
Async XLA Ops:
  0.6 72.7 %copy-start = (f32[1536]{0:T(1024)S(1)}, f32[1536]{0:T(1024)}, u32[]{:S(2)}) copy-start(f32[1536]{0:T(1024)} %param.11) | copy-start | bytes 18436
  37.1 36.1 %copy-start.1 = (s32[2048,2]{0,1:T(2,128)S(1)}, s32[2048,2]{0,1:T(2,128)}, u32[]{:S(2)}) copy-start(s32[2048,2]{0,1:T(2,128)} %param.9) | copy-start | bytes 49156
  37.1 37.7 %copy-start.2 = (s32[32,2]{0,1:T(2,128)S(1)}, s32[32,2]{0,1:T(2,128)}, u32[]{:S(2)}) copy-start(s32[32,2]{0,1:T(2,128)} %param.8) | copy-start | bytes 772
  37.1 37.8 %copy-start.3 = (f32[128]{0:T(128)S(1)}, f32[128]{0:T(128)}, u32[]{:S(2)}) copy-start(f32[128]{0:T(128)} %param.10) | copy-start | bytes 1540

commit v15 on v13

--- a/solution.py
+++ b/solution.py
@@ -262,7 +262,7 @@
             ring_copy(1, s, q).wait_send()
 
 
-def scatter_rows(partial_value, n_cd, n_chunks=4):
+def scatter_rows(partial_value, n_cd, n_chunks=2):
     n_y = n_cd // 2
     total_rows, cols = partial_value.shape
     rows = total_rows // n_cd

time: 77.5 us -> 79.1 us (1.021); the launches traced: 77.2 us -> 77.5 us
  no operation moved by 1% of the time
where the time goes in v15:
time: 79.1 us; the launch traced here: 77.5 us
  Pallas kernels  64.9 us (82%)
  matrix products  9.85 us (12%)
  other arithmetic  1.99 us (3%)
    pallas_call x1, Pallas kernels, scatter_rows(): pl.pallas_call(functools.partial(scatter_kernel, n_y, n_chunks), out_shap...  36.4 us
    pallas_call x1, Pallas kernels, gather_rows(): pl.pallas_call(functools.partial(gather_kernel, n_x, n_z), out_shape=jax....  28.5 us
    dot_general x1, matrix products, contract_rows(): lax.dot_general(row_block, col_block, (((1,), (1,)), ((), ())), precision...  7.98 us
    select_n x1, other arithmetic, on_device(): return (jnp.where(denominator == denominator, ladder, update), update)  1.89 us
    dot_general x4, matrix products, lookup_energy(): lax.dot_general(one_hot, table, (((1,), (1,)), ((), ())), precision=lax.P...  1.86 us

profile of v15, /device:TPU:1, one launch (start us, length us, event | category | flops | bytes accessed | tf_op | source)
XLA Modules:
  0.0 77.5 jit_solution(18230968507545911851)
XLA Ops:
  0.6 0.0 copy-start
  0.6 28.5 %shard_map.77 = f32[512,512]{1,0:T(8,128)} custom-call(f32[16,512]{1,0:T(8,128)} %amp_ref.1), custom_call_target="tpu_custom_call" | custom-call | tf_op jit(solution)/shard_map/pallas_call | solution.py:135
  29.2 8.0 %fusion.21 = f32[512,2048]{1,0:T(8,128)} fusion(f32[512,512]{1,0:T(8,128)} %shard_map.77, f32[2048,512]{1,0:T(8,128)} %param.7), kind=kOutput, calls=%fused_computation.53 | convolution fusion | flops 3221225472 | bytes 9437184 | tf_op jit(solution)/shard_map/dot_general | solution.py:29
  37.1 0.0 copy-start.1
  37.2 0.0 copy-start.2
  37.2 0.0 copy-start.3
  37.2 36.4 %shard_map.78 = f32[32,2048]{1,0:T(8,128)} custom-call(f32[8,2,32,2048]{3,2,1,0:T(8,128)} %bitcast.50), custom_call_target="tpu_custom_call" | custom-call | tf_op jit(solution)/shard_map/pallas_call | solution.py:272
  73.6 0.0 copy-done.1
  73.6 0.1 and_select_fusion.1
  73.7 0.0 copy-done
  73.7 0.7 fusion.1
  74.4 0.7 fusion
  75.2 0.0 copy-done.2
  75.2 0.0 copy-done.3
  75.2 0.2 fusion.2
  75.4 0.2 fusion.4
  75.6 1.9 %fusion.9 = (f32[32,2048]{1,0:T(8,128)}, f32[32,2048]{1,0:T(8,128)}) fusion(f32[32,2048]{1,0:T(8,128)} %shard_map.78, f32[2048]{0:T(1024)S(1)} %fusion.1, f32[2048]{0:T(1024)S(1)} %fusion, f32[32]{0:T(128)S(1)} %fusion.4), kind=kLoop, calls=%fused_computation.16 | loop fusion | flops 327680 | bytes 802944 | tf_op jit(solution)/shard_map/jit(_where)/select_n | solution.py:303
  (1 shorter events, 0.0 us)
Async XLA Ops:
  0.6 73.0 %copy-start = (f32[1536]{0:T(1024)S(1)}, f32[1536]{0:T(1024)}, u32[]{:S(2)}) copy-start(f32[1536]{0:T(1024)} %param.11) | copy-start | bytes 18436
  37.1 36.4 %copy-start.1 = (s32[2048,2]{0,1:T(2,128)S(1)}, s32[2048,2]{0,1:T(2,128)}, u32[]{:S(2)}) copy-start(s32[2048,2]{0,1:T(2,128)} %param.9) | copy-start | bytes 49156
  37.2 38.0 %copy-start.2 = (s32[32,2]{0,1:T(2,128)S(1)}, s32[32,2]{0,1:T(2,128)}, u32[]{:S(2)}) copy-start(s32[32,2]{0,1:T(2,128)} %param.8) | copy-start | bytes 772
  37.2 38.0 %copy-start.3 = (f32[128]{0:T(128)S(1)}, f32[128]{0:T(128)}, u32[]{:S(2)}) copy-start(f32[128]{0:T(128)} %param.10) | copy-start | bytes 1540

commit v16 on v13

--- a/solution.py
+++ b/solution.py
@@ -292,12 +292,15 @@
 
 
 def on_device(n_x, n_z, n_cd, amplitudes, integrals, ij_pairs, ab_pairs, eps_occ, eps_vir):
-    partial_value = contract_rows(gather_rows(amplitudes, n_x, n_z), integrals)
-    ladder = scatter_rows(partial_value, n_cd)
     first_occ = lookup_energy(ij_pairs[:, 0], eps_occ)[:, None]
     second_occ = lookup_energy(ij_pairs[:, 1], eps_occ)[:, None]
     first_vir = lookup_energy(ab_pairs[:, 0], eps_vir)[None, :]
     second_vir = lookup_energy(ab_pairs[:, 1], eps_vir)[None, :]
+    first_occ, second_occ, first_vir, second_vir, amplitudes = lax.optimization_barrier(
+        (first_occ, second_occ, first_vir, second_vir, amplitudes)
+    )
+    partial_value = contract_rows(gather_rows(amplitudes, n_x, n_z), integrals)
+    ladder = scatter_rows(partial_value, n_cd)
     denominator = first_occ + second_occ - first_vir - second_vir
     update = ladder / denominator
     return (jnp.where(denominator == denominator, ladder, update), update)

time: 77.5 us -> 80.2 us (1.035)
  other arithmetic: 1.99 us -> 3.53 us
  matrix products: 9.85 us -> 11.2 us
    dot_general x4, matrix products: 1.86 us -> 3.25 us  [lookup_energy(): lax.dot_general(one_hot, table, (((1,), (1,)), ((), ())), precision=lax.P...]
    select_n x1, other arithmetic: 0.08 us -> 0.89 us  [lookup_energy(): high = indices // lanes]
where the time goes in v16:
time: 80.2 us; the launch traced here: 79.8 us
  Pallas kernels  64.3 us (80%)
  matrix products  11.2 us (14%)
  other arithmetic  3.53 us (4%)
    pallas_call x1, Pallas kernels, scatter_rows(): pl.pallas_call(functools.partial(scatter_kernel, n_y, n_chunks), out_shap...  35.9 us
    pallas_call x1, Pallas kernels, gather_rows(): pl.pallas_call(functools.partial(gather_kernel, n_x, n_z), out_shape=jax....  28.4 us
    dot_general x1, matrix products, contract_rows(): lax.dot_general(row_block, col_block, (((1,), (1,)), ((), ())), precision...  7.97 us
    dot_general x4, matrix products, lookup_energy(): lax.dot_general(one_hot, table, (((1,), (1,)), ((), ())), precision=lax.P...  3.25 us
    select_n x1, other arithmetic, on_device(): return (jnp.where(denominator == denominator, ladder, update), update)  1.87 us

profile of v16, /device:TPU:1, one launch (start us, length us, event | category | flops | bytes accessed | tf_op | source)
XLA Modules:
  0.0 79.8 jit_solution(3231613185279947729)
XLA Ops:
  0.6 0.0 copy-start
  0.6 0.8 fusion.18
  1.4 0.9 %fusion.5 = f32[32,1]{0,1:T(1,128)S(1)} fusion(s32[32]{0:T(128)S(1)} %get-tuple-element.20, f32[128]{0:T(128)} %param.10, s32[32,2]{0,1:T(2,128)} %param.8), kind=kOutput, calls=%fused_computation.9 | convolution fusion | flops 53792 | bytes 896 | tf_op jit(solution)/shard_map/dot_general | solution.py:20
  2.3 0.9 %fusion.4 = f32[32,1]{0,1:T(1,128)S(1)} fusion(s32[32]{0:T(128)S(1)} %get-tuple-element.21, f32[128]{0:T(128)} %param.10, s32[32,2]{0,1:T(2,128)} %param.8), kind=kOutput, calls=%fused_computation.8 | convolution fusion | flops 53792 | bytes 896 | tf_op jit(solution)/shard_map/dot_general | solution.py:20
  3.2 0.9 %and_select_fusion = (s32[2048,1]{0,1:T(1,128)S(1)}, s32[2048,1]{0,1:T(1,128)S(1)}, s32[2048,1]{0,1:T(1,128)S(1)}, s32[2048,1]{0,1:T(1,128)S(1)}) fusion(s32[2048,2]{0,1:T(2,128)} %param.9), kind=kLoop, calls=%fused_computation.20 | loop fusion | flops 61440 | bytes 49152 | tf_op jit(solution)/shard_map/jit(floor_divide)/jit(_where)/select_n | solution.py:18
  4.1 0.0 copy-done
  4.1 0.7 fusion.1
  4.8 0.7 fusion
  5.6 28.4 %shard_map.77 = f32[512,512]{1,0:T(8,128)} custom-call(f32[16,512]{1,0:T(8,128)} %amp_ref), custom_call_target="tpu_custom_call" | custom-call | tf_op jit(solution)/shard_map/pallas_call | solution.py:135
  34.0 8.0 %fusion.22 = f32[512,2048]{1,0:T(8,128)} fusion(f32[512,512]{1,0:T(8,128)} %shard_map.77, f32[2048,512]{1,0:T(8,128)} %param.7), kind=kOutput, calls=%fused_computation.55 | convolution fusion | flops 3221225472 | bytes 9437184 | tf_op jit(solution)/shard_map/dot_general | solution.py:29
  42.0 35.9 %shard_map.78 = f32[32,2048]{1,0:T(8,128)} custom-call(f32[8,2,32,2048]{3,2,1,0:T(8,128)} %bitcast.64), custom_call_target="tpu_custom_call" | custom-call | tf_op jit(solution)/shard_map/pallas_call | solution.py:272
  77.9 1.9 %fusion.10 = (f32[32,2048]{1,0:T(8,128)}, f32[32,2048]{1,0:T(8,128)}) fusion(f32[32,2048]{1,0:T(8,128)} %shard_map.78, f32[2048]{0:T(1024)S(1)} %fusion.1, f32[2048]{0:T(1024)S(1)} %fusion, f32[32]{0:T(128)S(1)} %add_bitcast_fusion), kind=kLoop, calls=%fused_computation.17 | loop fusion | flops 327680 | bytes 802944 | tf_op jit(solution)/shard_map/jit(_where)/select_n | solution.py:306
  (1 shorter events, 0.0 us)
Async XLA Ops:
  0.6 3.5 %copy-start = (f32[1536]{0:T(1024)S(1)}, f32[1536]{0:T(1024)}, u32[]{:S(2)}) copy-start(f32[1536]{0:T(1024)} %param.11) | copy-start | bytes 18436

commit v17 on v13

--- a/solution.py
+++ b/solution.py
@@ -179,7 +179,8 @@
             if k % n_y not in [j % n_y for j in fetch_order]:
                 fetch_order.append(k)
     fetch_order.append(0)
-    for k in fetch_order:
+    early = fetch_order[:2]
+    for k in early:
         fetch(k).start()
 
     barrier = pltpu.get_barrier_semaphore()
@@ -206,6 +207,8 @@
 
     for k in order:
         pair_copy(k).start()
+        if k % n_y not in [j % n_y for j in early]:
+            fetch(k).start()
 
     def own(k, cols):
         b = lax.rem(y + k + n_y, n_y)

time: 77.5 us -> 77.5 us (level)
  no operation moved by 1% of the time
where the time goes in v17:
time: 77.5 us; the launch traced here: 77.2 us
  Pallas kernels  64.6 us (83%)
  matrix products  9.85 us (13%)
  other arithmetic  1.99 us (3%)
    pallas_call x1, Pallas kernels, scatter_rows(): pl.pallas_call(functools.partial(scatter_kernel, n_y, n_chunks), out_shap...  36.1 us
    pallas_call x1, Pallas kernels, gather_rows(): pl.pallas_call(functools.partial(gather_kernel, n_x, n_z), out_shape=jax....  28.5 us
    dot_general x1, matrix products, contract_rows(): lax.dot_general(row_block, col_block, (((1,), (1,)), ((), ())), precision...  7.98 us
    select_n x1, other arithmetic, on_device(): return (jnp.where(denominator == denominator, ladder, update), update)  1.89 us
    dot_general x4, matrix products, lookup_energy(): lax.dot_general(one_hot, table, (((1,), (1,)), ((), ())), precision=lax.P...  1.86 us

profile of v17, /device:TPU:1, one launch (start us, length us, event | category | flops | bytes accessed | tf_op | source)
XLA Modules:
  0.0 77.2 jit_solution(2701944721800213956)
XLA Ops:
  0.6 0.0 copy-start
  0.6 28.5 %shard_map.77 = f32[512,512]{1,0:T(8,128)} custom-call(f32[16,512]{1,0:T(8,128)} %amp_ref.1), custom_call_target="tpu_custom_call" | custom-call | tf_op jit(solution)/shard_map/pallas_call | solution.py:135
  29.2 8.0 %fusion.21 = f32[512,2048]{1,0:T(8,128)} fusion(f32[512,512]{1,0:T(8,128)} %shard_map.77, f32[2048,512]{1,0:T(8,128)} %param.7), kind=kOutput, calls=%fused_computation.53 | convolution fusion | flops 3221225472 | bytes 9437184 | tf_op jit(solution)/shard_map/dot_general | solution.py:29
  37.1 0.0 copy-start.1
  37.2 0.0 copy-start.2
  37.2 0.0 copy-start.3
  37.2 36.1 %shard_map.78 = f32[32,2048]{1,0:T(8,128)} custom-call(f32[8,2,32,2048]{3,2,1,0:T(8,128)} %bitcast.50), custom_call_target="tpu_custom_call" | custom-call | tf_op jit(solution)/shard_map/pallas_call | solution.py:275
  73.2 0.0 copy-done.1
  73.2 0.1 and_select_fusion.1
  73.3 0.0 copy-done
  73.3 0.7 fusion.1
  74.1 0.7 fusion
  74.8 0.0 copy-done.2
  74.9 0.0 copy-done.3
  74.9 0.2 fusion.2
  75.1 0.2 fusion.4
  75.3 1.9 %fusion.9 = (f32[32,2048]{1,0:T(8,128)}, f32[32,2048]{1,0:T(8,128)}) fusion(f32[32,2048]{1,0:T(8,128)} %shard_map.78, f32[2048]{0:T(1024)S(1)} %fusion.1, f32[2048]{0:T(1024)S(1)} %fusion, f32[32]{0:T(128)S(1)} %fusion.4), kind=kLoop, calls=%fused_computation.16 | loop fusion | flops 327680 | bytes 802944 | tf_op jit(solution)/shard_map/jit(_where)/select_n | solution.py:306
  (1 shorter events, 0.0 us)
Async XLA Ops:
  0.6 72.7 %copy-start = (f32[1536]{0:T(1024)S(1)}, f32[1536]{0:T(1024)}, u32[]{:S(2)}) copy-start(f32[1536]{0:T(1024)} %param.11) | copy-start | bytes 18436
  37.1 36.1 %copy-start.1 = (s32[2048,2]{0,1:T(2,128)S(1)}, s32[2048,2]{0,1:T(2,128)}, u32[]{:S(2)}) copy-start(s32[2048,2]{0,1:T(2,128)} %param.9) | copy-start | bytes 49156
  37.2 37.7 %copy-start.2 = (s32[32,2]{0,1:T(2,128)S(1)}, s32[32,2]{0,1:T(2,128)}, u32[]{:S(2)}) copy-start(s32[32,2]{0,1:T(2,128)} %param.8) | copy-start | bytes 772
  37.2 37.7 %copy-start.3 = (f32[128]{0:T(128)S(1)}, f32[128]{0:T(128)}, u32[]{:S(2)}) copy-start(f32[128]{0:T(128)} %param.10) | copy-start | bytes 1540

commit v18 on v13

--- a/solution.py
+++ b/solution.py
@@ -294,10 +294,13 @@
 def on_device(n_x, n_z, n_cd, amplitudes, integrals, ij_pairs, ab_pairs, eps_occ, eps_vir):
     partial_value = contract_rows(gather_rows(amplitudes, n_x, n_z), integrals)
     ladder = scatter_rows(partial_value, n_cd)
-    first_occ = lookup_energy(ij_pairs[:, 0], eps_occ)[:, None]
-    second_occ = lookup_energy(ij_pairs[:, 1], eps_occ)[:, None]
-    first_vir = lookup_energy(ab_pairs[:, 0], eps_vir)[None, :]
-    second_vir = lookup_energy(ab_pairs[:, 1], eps_vir)[None, :]
+    n_ij, n_ab = ij_pairs.shape[0], ab_pairs.shape[0]
+    occ = lookup_energy(jnp.concatenate([ij_pairs[:, 0], ij_pairs[:, 1]]), eps_occ)
+    vir = lookup_energy(jnp.concatenate([ab_pairs[:, 0], ab_pairs[:, 1]]), eps_vir)
+    first_occ = occ[:n_ij][:, None]
+    second_occ = occ[n_ij:][:, None]
+    first_vir = vir[:n_ab][None, :]
+    second_vir = vir[n_ab:][None, :]
     denominator = first_occ + second_occ - first_vir - second_vir
     update = ladder / denominator
     return (jnp.where(denominator == denominator, ladder, update), update)

time: 77.5 us -> 77.5 us (level)
    dot_general x4 -> x2, matrix products: 1.86 us -> 1.69 us  [lookup_energy(): lax.dot_general(one_hot, table, (((1,), (1,)), ((), ())), precision=lax.P...]
where the time goes in v18:
time: 77.5 us; the launch traced here: 77.2 us
  Pallas kernels  64.7 us (83%)
  matrix products  9.67 us (12%)
  other arithmetic  2.07 us (3%)
    pallas_call x1, Pallas kernels, scatter_rows(): pl.pallas_call(functools.partial(scatter_kernel, n_y, n_chunks), out_shap...  36.1 us
    pallas_call x1, Pallas kernels, gather_rows(): pl.pallas_call(functools.partial(gather_kernel, n_x, n_z), out_shape=jax....  28.5 us
    dot_general x1, matrix products, contract_rows(): lax.dot_general(row_block, col_block, (((1,), (1,)), ((), ())), precision...  7.98 us
    select_n x1, other arithmetic, on_device(): return (jnp.where(denominator == denominator, ladder, update), update)  1.9 us
    dot_general x2, matrix products, lookup_energy(): lax.dot_general(one_hot, table, (((1,), (1,)), ((), ())), precision=lax.P...  1.69 us

profile of v18, /device:TPU:1, one launch (start us, length us, event | category | flops | bytes accessed | tf_op | source)
XLA Modules:
  0.0 77.2 jit_solution(7981099024817573820)
XLA Ops:
  0.6 0.0 copy-start
  0.6 28.5 %shard_map.77 = f32[512,512]{1,0:T(8,128)} custom-call(f32[16,512]{1,0:T(8,128)} %amp_ref.1), custom_call_target="tpu_custom_call" | custom-call | tf_op jit(solution)/shard_map/pallas_call | solution.py:135
  29.2 8.0 %fusion.13 = f32[512,2048]{1,0:T(8,128)} fusion(f32[512,512]{1,0:T(8,128)} %shard_map.77, f32[2048,512]{1,0:T(8,128)} %param.7), kind=kOutput, calls=%fused_computation.32 | convolution fusion | flops 3221225472 | bytes 9437184 | tf_op jit(solution)/shard_map/dot_general | solution.py:29
  37.2 0.0 copy-start.1
  37.2 0.0 copy-start.2
  37.2 0.0 copy-start.3
  37.2 36.1 %shard_map.78 = f32[32,2048]{1,0:T(8,128)} custom-call(f32[8,2,32,2048]{3,2,1,0:T(8,128)} %bitcast.19), custom_call_target="tpu_custom_call" | custom-call | tf_op jit(solution)/shard_map/pallas_call | solution.py:272
  73.3 0.0 copy-done.1
  73.4 0.0 copy-done
  73.4 1.5 %fusion = f32[4096]{0:T(1024)S(1)} fusion(s32[4096]{0:T(1024)S(1)} %get-tuple-element.7, s32[4096]{0:T(1024)S(1)} %get-tuple-element.6, f32[1536]{0:T(1024)S(1)} %copy-done), kind=kOutput, calls=%fused_computation.2 | convolution fusion | flops 76165120 | bytes 55296 | tf_op jit(solution)/shard_map/dot_general | solution.py:20
  74.9 0.0 copy-done.2
  74.9 0.1 compare_select_fusion.1
  75.0 0.0 copy-done.3
  75.0 0.2 fusion.1
  75.2 0.1 slice_add_fusion
  75.3 1.9 %fusion.5 = (f32[32,2048]{1,0:T(8,128)}, f32[32,2048]{1,0:T(8,128)}) fusion(f32[32,2048]{1,0:T(8,128)} %shard_map.78, f32[2048]{0:T(1024)S(1)} %get-tuple-element.5, f32[2048]{0:T(1024)S(1)} %get-tuple-element.4, f32[32]{0:T(128)S(1)} %slice_add_fusion), kind=kLoop, calls=%fused_computation.10 | loop fusion | flops 327680 | bytes 802944 | tf_op jit(solution)/shard_map/jit(_where)/select_n | solution.py:306
  (4 shorter events, 0.0 us)
Async XLA Ops:
  0.6 72.7 %copy-start = (f32[1536]{0:T(1024)S(1)}, f32[1536]{0:T(1024)}, u32[]{:S(2)}) copy-start(f32[1536]{0:T(1024)} %param.11) | copy-start | bytes 18436
  37.2 36.2 %copy-start.1 = (s32[2048,2]{0,1:T(2,128)S(1)}, s32[2048,2]{0,1:T(2,128)}, u32[]{:S(2)}) copy-start(s32[2048,2]{0,1:T(2,128)} %param.9) | copy-start | bytes 49156
  37.2 37.7 %copy-start.2 = (s32[32,2]{0,1:T(2,128)S(1)}, s32[32,2]{0,1:T(2,128)}, u32[]{:S(2)}) copy-start(s32[32,2]{0,1:T(2,128)} %param.8) | copy-start | bytes 772
  37.2 37.8 %copy-start.3 = (f32[128]{0:T(128)S(1)}, f32[128]{0:T(128)}, u32[]{:S(2)}) copy-start(f32[128]{0:T(128)} %param.10) | copy-start | bytes 1540
